TPU v7x, 128 devices: a whole 4x4x4 slice. The times are simulated.
128 devices in a mesh: store: 64 (over x, y, z), rep: 2 (over core).
Axes of the slice: x: 4, y: 4, z: 4, core: 2. Of those that a mesh axis runs over, the one named last changes fastest.
Arguments:
- features: bfloat16 [131072, 768], P('store'), may hold values from -6 to 6
- owners_near: int32 [65536, 1], P(('store', 'rep')), may hold values from 0 to 63; in each aligned block of 512 rows (0 to 511, 512 to 1023, ...) at most 16 rows name the same one
- slots_near: int32 [65536, 1], P(('store', 'rep')), may hold values from 0 to 2047
- owners_far: int32 [393216, 1], P(('store', 'rep')), may hold values from 0 to 63; in each aligned block of 3072 rows (0 to 3071, 3072 to 6143, ...) at most 96 rows name the same one
- slots_far: int32 [393216, 1], P(('store', 'rep')), may hold values from 0 to 2047
- adjacency_low: int32 [65536, 15], P(('store', 'rep')), may hold values from 0 to 3583
- adjacency_top: int32 [16384, 10], P(('store', 'rep')), may hold values from 0 to 511
- labels: int32 [16384], P(('store', 'rep')), may hold values from 0 to 152
- weights_low: float32 [1536, 1024], replicated, may hold values from -0.15625 to 0.15625
- weights_top: float32 [2048, 153], replicated, may hold values from -0.25 to 0.25
- first_low: float32 [1536, 1024], P(('store', 'rep')), may hold values from -0.00390625 to 0.00390625
- second_low: float32 [1536, 1024], P(('store', 'rep')), may hold values from 1e-09 to 1e-07
- first_top: float32 [2048, 153], P(('store', 'rep')), may hold values from -0.03125 to 0.03125
- second_top: float32 [2048, 153], P(('store', 'rep')), may hold values from 1e-07 to 1e-05
Outputs:
- logits: float32 [16384, 153], P(('store', 'rep'))
- new_low: float32 [1536, 1024], replicated
- new_first_low: float32 [1536, 1024], P(('store', 'rep'))
- new_second_low: float32 [1536, 1024], P(('store', 'rep'))
- new_top: float32 [2048, 153], replicated
- new_first_top: float32 [2048, 153], P(('store', 'rep'))
- new_second_top: float32 [2048, 153], P(('store', 'rep'))
Inputs may be any that keep to these rules, and one draw needn't show every extreme that they name: `owners_near`: within the rows of one trainer, no store index is named more than 16 times, and some index is named exactly that often. `owners_far`: within the rows of one trainer, no store index is named more than 96 times, and some index is named exactly that often.
All inputs are finite; a program needn't handle non-finite values.
Results may differ from a plain program's by a relative error of at most 0.005.
Values may be sent and summed in bfloat16 or wider, within the bound.
A program may use at most 128 MiB of HBM per device.

v0:
```python
import jax
import jax.numpy as jnp
from jax import lax
from jax.sharding import PartitionSpec as P

beta_one = 0.9
beta_two = 0.999
bias_one = 1.0 - 0.9**10
bias_two = 1.0 - 0.999**10
learn_rate = 0.01
adam_eps = 1e-08


def gelu_tanh(values):
    return jax.nn.gelu(values, approximate=True)


def local_step(fetched, adjacency_low, adjacency_top, labels, low_bf, top_bf, scale):
    near_rows = adjacency_low.shape[0]
    seed_rows = labels.shape[0]
    width = top_bf.shape[0] // 2
    classes_all = top_bf.shape[1]
    gathered = jnp.zeros((near_rows, fetched.shape[1]), jnp.float32)
    for column in range(adjacency_low.shape[1]):
        gathered = gathered + fetched[adjacency_low[:, column]].astype(jnp.float32)
    low_mean = (gathered / adjacency_low.shape[1]).astype(jnp.bfloat16)
    low_input = jnp.concatenate([fetched[:near_rows], low_mean], axis=1)
    pre_hidden = jnp.dot(low_input, low_bf, preferred_element_type=jnp.float32)
    hidden = gelu_tanh(pre_hidden).astype(jnp.bfloat16)
    top_sum = jnp.zeros((seed_rows, width), jnp.float32)
    for column in range(adjacency_top.shape[1]):
        top_sum = top_sum + hidden[adjacency_top[:, column]].astype(jnp.float32)
    top_mean = (top_sum / adjacency_top.shape[1]).astype(jnp.bfloat16)
    top_input = jnp.concatenate([hidden[:seed_rows], top_mean], axis=1)
    logits = jnp.dot(top_input, top_bf, preferred_element_type=jnp.float32)
    powers = jnp.exp(logits)
    chances = powers / jnp.sum(powers, axis=1, keepdims=True)
    targets = (labels[:, None] == jnp.arange(classes_all, dtype=jnp.int32)[None, :]).astype(
        jnp.float32
    )
    dlogits = ((chances - targets) * scale).astype(jnp.bfloat16)
    grad_top = lax.dot_general(
        top_input, dlogits, (((0,), (0,)), ((), ())), preferred_element_type=jnp.float32
    )
    dinput = lax.dot_general(
        dlogits, top_bf, (((1,), (1,)), ((), ())), preferred_element_type=jnp.float32
    )
    dhidden = jnp.zeros((near_rows, width), jnp.float32).at[:seed_rows].add(dinput[:, :width])
    spread = dinput[:, width:] / adjacency_top.shape[1]
    for column in range(adjacency_top.shape[1]):
        dhidden = dhidden.at[adjacency_top[:, column]].add(spread)
    unused, pullback = jax.vjp(gelu_tanh, pre_hidden)
    dpre = pullback(dhidden)[0].astype(jnp.bfloat16)
    grad_low = lax.dot_general(
        low_input, dpre, (((0,), (0,)), ((), ())), preferred_element_type=jnp.float32
    )
    return (logits, grad_low, grad_top)


def adam_update(weight, moment, square, gradient):
    moment_new = beta_one * moment + (1.0 - beta_one) * gradient
    square_new = beta_two * square + (1.0 - beta_two) * gradient * gradient
    update = moment_new / bias_one / (jnp.sqrt(square_new / bias_two) + adam_eps)
    return (weight - learn_rate * update, moment_new, square_new)


def bucket(owners, slots, stores, capacity):
    owner_marks = (owners[:, None] == jnp.arange(stores, dtype=jnp.int32)[None, :]).astype(
        jnp.int32
    )
    places = jnp.sum((jnp.cumsum(owner_marks, axis=0) - owner_marks) * owner_marks, axis=1)
    requests = jnp.zeros((stores, capacity), jnp.int32).at[owners, places].set(slots)
    return (requests, places)


def fetch_rows(owners, slots, capacity, table):
    stores = lax.axis_size("store")
    requests, places = bucket(owners, slots, stores, capacity)
    found = table[lax.all_to_all(requests, "store", split_axis=0, concat_axis=0, tiled=True)]
    arrived = lax.all_to_all(found, "store", split_axis=0, concat_axis=0, tiled=True)
    return arrived[owners, places]


def per_device(
    features,
    owners_near,
    slots_near,
    owners_far,
    slots_far,
    adjacency_low,
    adjacency_top,
    labels,
    weights_low,
    weights_top,
    first_low,
    second_low,
    first_top,
    second_top,
):
    stores = lax.axis_size("store")
    near_owners = owners_near[:, 0]
    far_owners = owners_far[:, 0]
    near_limit = 2 * near_owners.shape[0] // stores
    far_limit = 2 * far_owners.shape[0] // stores
    fetched = jnp.concatenate(
        [
            fetch_rows(near_owners, slots_near[:, 0], near_limit, features),
            fetch_rows(far_owners, slots_far[:, 0], far_limit, features),
        ],
        axis=0,
    )
    members = lax.axis_size(("store", "rep"))
    scale = 1.0 / (labels.shape[0] * members)
    logits, grad_low, grad_top = local_step(
        fetched,
        adjacency_low,
        adjacency_top,
        labels,
        weights_low.astype(jnp.bfloat16),
        weights_top.astype(jnp.bfloat16),
        scale,
    )
    position = lax.axis_index(("store", "rep"))
    rows_low = first_low.shape[0]
    rows_top = first_top.shape[0]
    whole_low, whole_top = lax.psum((grad_low, grad_top), ("store", "rep"))
    share_low = lax.dynamic_slice_in_dim(whole_low, position * rows_low, rows_low, 0)
    share_top = lax.dynamic_slice_in_dim(whole_top, position * rows_top, rows_top, 0)
    own_low = lax.dynamic_slice_in_dim(weights_low, position * rows_low, rows_low, 0)
    own_top = lax.dynamic_slice_in_dim(weights_top, position * rows_top, rows_top, 0)
    part_low, new_first_low, new_second_low = adam_update(own_low, first_low, second_low, share_low)
    part_top, new_first_top, new_second_top = adam_update(own_top, first_top, second_top, share_top)
    new_low, new_top = (
        lax.all_gather(part_low, ("store", "rep"), axis=0, tiled=True),
        lax.all_gather(part_top, ("store", "rep"), axis=0, tiled=True),
    )
    return (logits, new_low, new_first_low, new_second_low, new_top, new_first_top, new_second_top)


def solution(mesh):
    return jax.shard_map(
        per_device,
        mesh=mesh,
        in_specs=(
            P("store", None),
            P(("store", "rep"), None),
            P(("store", "rep"), None),
            P(("store", "rep"), None),
            P(("store", "rep"), None),
            P(("store", "rep"), None),
            P(("store", "rep"), None),
            P(("store", "rep")),
            P(),
            P(),
            P(("store", "rep"), None),
            P(("store", "rep"), None),
            P(("store", "rep"), None),
            P(("store", "rep"), None),
        ),
        out_specs=(
            P(("store", "rep"), None),
            P(),
            P(("store", "rep"), None),
            P(("store", "rep"), None),
            P(),
            P(("store", "rep"), None),
            P(("store", "rep"), None),
        ),
        check_vma=False,
    )
```

profile of v0, /device:TPU:1, one launch (start us, length us, event | category | flops | bytes accessed | tf_op | source)
XLA Modules:
  0.0 879.7 jit_solution(14029218526788005740)
XLA Ops:
  11.0 42.9 %scatter_fusion = s32[64,16]{0,1:T(8,128)S(1)} fusion(s32[64,16]{0,1:T(8,128)S(1)} %broadcast.218, s32[512]{0:T(512)S(1)} %bitcast.100, s32[512]{0:T(512)} %bitcast.128), kind=kCustom, calls=%fused_computation.29 | custom fusion | bytes 10240 | tf_op jit(solution)/shard_map/scatter | solution.py:72
  54.6 12.0 %all-to-all-start = ((s32[64,1,16]{2,1,0:T(1,128)}), s32[64,1,16]{2,1,0:T(1,128)S(1)}, u32[]{:S(2)}, u32[]{:S(2)}) async-start(s32[64,1,16]{2,1,0:T(1,128)} %copy.30), calls=%async_computation | async-start | bytes 65536 | tf_op jit(solution)/shard_map/all_to_all | solution.py:79
  67.5 34.9 %reduce-window.16 = s32[64,24,128]{2,1,0:T(8,128)} reduce-window(s32[64,24,128]{2,1,0:T(8,128)} %fusion.20, s32[]{:T(128)} %constant.42.clone.1), window={size=1x1x128 pad=0_0x0_0x127_0}, to_apply=%region_4.5 | reduce-window | flops 24969216 | bytes 1572868 | tf_op jit(solution)/shard_map/reduce-window.2
  102.4 2.3 slice.215
  104.7 1.6 copy.35
  106.5 1.4 broadcast_add_fusion
  108.4 12.0 %scatter_custom_fusion.11 = s32[6144]{0:T(1024)S(1)} fusion(s32[3072]{0:T(1024)S(1)} %broadcast_select_fusion, s32[3072]{0:T(1024)} %bitcast.129, s32[]{:T(128)} %constant.42.clone.1), kind=kCustom, calls=%fused_computation.107 | custom fusion | bytes 25088
  121.2 9.8 %all-to-all-start.2 = ((s32[64,1,96]{2,1,0:T(1,128)}), s32[64,1,96]{2,1,0:T(1,128)S(1)}, u32[]{:S(2)}, u32[]{:S(2)}) async-start(s32[64,1,96]{2,1,0:T(1,128)} %all_to_all.26), calls=%async_computation.2 | async-start | bytes 65536 | tf_op jit(solution)/shard_map/all_to_all | solution.py:79
  131.1 5.2 gather_fusion
  136.3 3.0 all-to-all-done.2
  139.3 7.0 all-to-all-start.1
  146.4 26.1 %gather_fusion.2 = bf16[6144,768]{1,0:T(8,128)(2,1)} fusion(bf16[2048,768]{1,0:T(8,128)(2,1)S(1)} %copy-done, s32[6144]{0:T(1024)S(1)} %broadcast_clamp_fusion), kind=kCustom, calls=%fused_computation.2 | custom fusion | bytes 18898944 | tf_op jit(solution)/shard_map/gather | solution.py:79
  172.6 10.1 %all-to-all-start.3 = ((bf16[64,96,768]{2,1,0:T(8,128)(2,1)}), bf16[64,96,768]{2,1,0:T(8,128)(2,1)}, u32[]{:S(2)}, u32[]{:S(2)}) async-start(bf16[64,96,768]{2,1,0:T(8,128)(2,1)} %bitcast.98), calls=%async_computation.3 | async-start | bytes 18874368 | tf_op jit(solution)/shard_map/all_to_all | solution.py:80
  183.4 7.5 gather_fusion.1
  191.9 116.7 %all-to-all-done.3 = bf16[64,96,768]{2,1,0:T(8,128)(2,1)} async-done(((bf16[64,96,768]{2,1,0:T(8,128)(2,1)}), bf16[64,96,768]{2,1,0:T(8,128)(2,1)}, u32[]{:S(2)}, u32[]{:S(2)}) %all-to-all-start.3) | async-done | bytes 9437216 | tf_op jit(solution)/shard_map/all_to_all | solution.py:80
  308.6 57.6 %gather_fusion.3 = bf16[3072,768]{1,0:T(8,128)(2,1)} fusion(bf16[64,96,768]{2,1,0:T(8,128)(2,1)} %all-to-all-done.3, s32[3072]{0:T(1024)S(1)} %bitcast.97), kind=kCustom, calls=%fused_computation.3 | custom fusion | bytes 9461760 | tf_op jit(solution)/shard_map/gather | solution.py:81
  366.2 4.8 constant_dynamic-update-slice_fusion
  371.0 5.7 gather_fusion.10
  376.7 5.7 gather_fusion.11
  382.4 5.7 gather_fusion.12
  388.0 6.3 gather_fusion.13
  394.4 6.4 gather_fusion.14
  400.7 6.5 gather_fusion.15
  407.3 6.4 gather_fusion.16
  413.7 6.3 gather_fusion.17
  420.0 6.3 gather_fusion.5
  426.4 6.4 gather_fusion.6
  432.7 6.4 gather_fusion.7
  439.1 6.4 gather_fusion.8
  445.4 6.3 gather_fusion.9
  451.8 6.3 gather_fusion.18
  458.1 6.8 gather_fusion.4
  464.9 5.2 multiply_convert_fusion.1
  470.2 6.5 multiply_convert_fusion
  476.7 1.5 gather_fusion.19
  478.3 1.6 gather_fusion.20
  479.8 1.6 gather_fusion.21
  481.4 1.6 gather_fusion.22
  483.0 1.6 gather_fusion.23
  484.5 1.6 gather_fusion.24
  486.1 1.6 gather_fusion.25
  487.7 1.6 gather_fusion.26
  489.3 1.6 gather_fusion.27
  490.8 1.6 gather_fusion.28
  492.4 2.1 multiply_convert_fusion.2
  494.9 1.8 fusion.21
  497.1 1.6 scatter-add.75
  498.7 4.5 scatter_custom_fusion.1
  503.2 4.5 scatter_custom_fusion.2
  507.6 4.5 scatter_custom_fusion.3
  512.1 4.5 scatter_custom_fusion.4
  516.6 4.7 scatter_custom_fusion.5
  521.2 4.5 scatter_custom_fusion.6
  525.7 4.5 scatter_custom_fusion.7
  530.2 4.5 scatter_custom_fusion.8
  534.7 4.5 scatter_custom_fusion.9
  539.2 4.5 scatter_custom_fusion.10
  543.6 7.3 fusion.9
  551.2 173.4 %all-reduce.4.cloned.1.call-done = (f32[1536,1024]{1,0:T(8,128)}, f32[2048,153]{1,0:T(8,128)}) async-done(((f32[1536,1024]{1,0:T(8,128)}, f32[2048,153]{1,0:T(8,128)}), (f32[1536,1024]{1,0:T(8,128)}, f32[2048,153]{1,0:T(8,128)})) %all-reduce.4.cloned.1.call-update) | async-done | bytes 7544848 | tf_op jit(solution)/shard_map/psum | solution.py:126
  726.0 1.6 subtract_bitcast_fusion
  727.7 65.2 %all-gather.4.cloned.1.call-done = f32[2048,153]{1,0:T(8,128)} async-done(((f32[16,153]{1,0:T(8,128)}), f32[2048,153]{1,0:T(8,128)}) %all-gather.4.cloned.1.call-update) | async-done | bytes 1253392 | tf_op jit(solution)/shard_map/all_gather | solution.py:135
  792.9 2.7 copy.34
  795.6 68.9 %all-gather.6.cloned.1.call-done = f32[128,12,1024]{2,1,0:T(8,128)} async-done(((f32[1,12,1024]{2,1,0:T(8,128)}), f32[128,12,1024]{2,1,0:T(8,128)}) %all-gather.6.cloned.1.call-update) | async-done | bytes 6291472 | tf_op jit(solution)/shard_map/all_gather | solution.py:134
  864.5 8.4 reshape.490
  (84 shorter events, 11.1 us)
Async XLA Ops:
  7.2 123.9 %copy-start = (bf16[2048,768]{1,0:T(8,128)(2,1)S(1)}, bf16[2048,768]{1,0:T(8,128)(2,1)}, u32[]{:S(2)}) copy-start(bf16[2048,768]{1,0:T(8,128)(2,1)} %param.16) | copy-start | bytes 9437188
  11.0 55.6 %copy-start.5 = (s32[3072,1]{0,1:T(1,128)S(1)}, s32[3072,1]{0,1:T(1,128)}, u32[]{:S(2)}) copy-start(s32[3072,1]{0,1:T(1,128)} %param.19) | copy-start | bytes 36868
  54.6 66.5 %all-to-all-start = ((s32[64,1,16]{2,1,0:T(1,128)}), s32[64,1,16]{2,1,0:T(1,128)S(1)}, u32[]{:S(2)}, u32[]{:S(2)}) async-start(s32[64,1,16]{2,1,0:T(1,128)} %copy.30), calls=%async_computation | async-start | bytes 65536 | tf_op jit(solution)/shard_map/all_to_all | solution.py:79
  102.4 5.8 copy-start.14
  104.7 3.6 copy-start.13
  121.2 18.1 %all-to-all-start.2 = ((s32[64,1,96]{2,1,0:T(1,128)}), s32[64,1,96]{2,1,0:T(1,128)S(1)}, u32[]{:S(2)}, u32[]{:S(2)}) async-start(s32[64,1,96]{2,1,0:T(1,128)} %all_to_all.26), calls=%async_computation.2 | async-start | bytes 65536 | tf_op jit(solution)/shard_map/all_to_all | solution.py:79
  139.3 33.3 %all-to-all-start.1 = ((bf16[64,16,768]{2,1,0:T(8,128)(2,1)}), bf16[64,16,768]{2,1,0:T(8,128)(2,1)}, u32[]{:S(2)}, u32[]{:S(2)}) async-start(bf16[64,16,768]{2,1,0:T(8,128)(2,1)} %bitcast.101), calls=%async_computation.1 | async-start | bytes 3145728 | tf_op jit(solution)/shard_map/all_to_all | solution.py:80
  172.6 10.6 %copy-start.8 = (s32[512,15]{0,1:T(8,128)S(1)}, s32[512,15]{0,1:T(8,128)}, u32[]{:S(2)}) copy-start(s32[512,15]{0,1:T(8,128)} %param.21) | copy-start | bytes 92164
  172.6 10.8 %copy-start.11 = (s32[128,10]{0,1:T(8,128)S(1)}, s32[128,10]{0,1:T(8,128)}, u32[]{:S(2)}) copy-start(s32[128,10]{0,1:T(8,128)} %param.22) | copy-start | bytes 15364
  172.6 136.1 %all-to-all-start.3 = ((bf16[64,96,768]{2,1,0:T(8,128)(2,1)}), bf16[64,96,768]{2,1,0:T(8,128)(2,1)}, u32[]{:S(2)}, u32[]{:S(2)}) async-start(bf16[64,96,768]{2,1,0:T(8,128)(2,1)} %bitcast.98), calls=%async_computation.3 | async-start | bytes 18874368 | tf_op jit(solution)/shard_map/all_to_all | solution.py:80
  182.7 541.9 %all-reduce.4.cloned.1.call-start = ((), (), s32[]{:S(2)}) async-start(), calls=%async_computation.6 | async-start | bytes 16777216 | tf_op jit(solution)/shard_map/psum | solution.py:126
  470.1 6.6 copy-start.3
  490.8 3.7 copy-start.2
  492.4 2.5 copy-start.12
  494.9 2.2 copy-start.4
  551.0 173.6 %copy-start.9 = (f32[16,153]{1,0:T(8,128)S(1)}, f32[16,153]{1,0:T(8,128)}, u32[]{:S(2)}) copy-start(f32[16,153]{1,0:T(8,128)} %param.28) | copy-start | bytes 29380
  551.0 173.6 %copy-start.10 = (f32[16,153]{1,0:T(8,128)S(1)}, f32[16,153]{1,0:T(8,128)}, u32[]{:S(2)}) copy-start(f32[16,153]{1,0:T(8,128)} %param.29) | copy-start | bytes 29380
  551.0 175.1 %copy-start.6 = (f32[12,1024]{1,0:T(8,128)S(1)}, f32[12,1024]{1,0:T(8,128)}, u32[]{:S(2)}) copy-start(f32[12,1024]{1,0:T(8,128)} %param.26) | copy-start | bytes 147460
  551.0 175.1 %copy-start.7 = (f32[12,1024]{1,0:T(8,128)S(1)}, f32[12,1024]{1,0:T(8,128)}, u32[]{:S(2)}) copy-start(f32[12,1024]{1,0:T(8,128)} %param.27) | copy-start | bytes 147460
  551.0 241.9 %all-gather.4.cloned.1.call-start = ((), (), s32[]{:S(2)}) async-start(), calls=%async_computation.4 | async-start | bytes 2113536 | tf_op jit(solution)/shard_map/all_gather | solution.py:135
  726.0 138.6 %all-gather.6.cloned.1.call-start = ((), (), s32[]{:S(2)}) async-start(), calls=%async_computation.5 | async-start | bytes 8454144 | tf_op jit(solution)/shard_map/all_gather | solution.py:134
  864.5 8.4 copy-start.1
Sparse Core Ops, SparseCore 0:
  551.1 173.4 all-reduce.3
  728.8 64.1 all-gather.3
  796.9 67.5 all-gather.5
where the time goes:
time: 892 us; the launch traced here: 880 us
  waiting for transfers between devices  427 us (48%)
  local copies, waits for them, and re-layouts  285 us (32%)
  other arithmetic  97 us (11%)
  starting transfers between devices  39.4 us (4%)
  matrix products  16.4 us (2%)
  between operations  14.4 us (2%)
    psum x1, waiting for transfers between devices, per_device(): whole_low, whole_top = lax.psum((grad_low, grad_top), ('store', 'rep'))  173 us
    all_to_all x2, waiting for transfers between devices, fetch_rows(): lax.all_to_all(found, 'store', split_axis=0, concat_axis=0, tiled=True)  117 us
    gather x15, local copies, waits for them, and re-layouts, local_step(): gathered = gathered + fetched[adjacency_low[:, column]].astype(jnp.float32)  93.8 us
    all_gather x1, waiting for transfers between devices, per_device(): lax.all_gather(part_low, ('store', 'rep'), axis=0, tiled=True)  68.9 us
    all_gather x1, waiting for transfers between devices, per_device(): lax.all_gather(part_top, ('store', 'rep'), axis=0, tiled=True)  65.2 us
    gather x2, local copies, waits for them, and re-layouts, fetch_rows(): return arrived[owners, places]  65.1 us
    scatter-add x10, other arithmetic, local_step(): dhidden = dhidden.at[adjacency_top[:, column]].add(spread)  45 us
    scatter x1, local copies, waits for them, and re-layouts, bucket(): jnp.zeros((stores, capacity), jnp.int32).at[owners, places].set(slots)  42.9 us
  transfers between devices with their start and end apart: 7, of which 5 were waited for; matrix products, arithmetic and copies ran while one was open for 11% of the time, Pallas kernels for 0%

commit v1 on v0

v1 whole, which is shorter than its diff:
```python
import functools

import jax
import jax.numpy as jnp
from jax import lax
from jax.experimental import pallas as pl
from jax.experimental.pallas import tpu as pltpu
from jax.sharding import PartitionSpec as P

beta_one = 0.9
beta_two = 0.999
bias_one = 1.0 - 0.9**10
bias_two = 1.0 - 0.999**10
learn_rate = 0.01
adam_eps = 1e-08

MESH = pl.DeviceIdType.MESH
F32 = jnp.float32
BF16 = jnp.bfloat16
SIDE = 4
STORES = SIDE**3
CAP_NEAR = 16
CAP_FAR = 96
CAP = CAP_NEAR + CAP_FAR
STRIDE, UNSTRIDE = 37, 45


def iota(shape, dim):
    return lax.broadcasted_iota(jnp.int32, shape, dim)


def dot(a, b):
    return jnp.dot(a, b, preferred_element_type=F32)


def dot_nt(a, b):
    return lax.dot_general(a, b, (((1,), (1,)), ((), ())), preferred_element_type=F32)


def place():
    store = lax.axis_index("store")
    rep = lax.axis_index("rep")
    return (store // 16, lax.rem(store // 4, 4), lax.rem(store, 4)), rep, 1 - 2 * rep


def partner(slot, chip, sign):
    shift = lax.rem(slot * STRIDE, STORES)
    steps = (shift // 16, lax.rem(shift // 4, 4), lax.rem(shift, 4))
    x, y, z = [lax.rem(at + sign * step + SIDE, SIDE) for at, step in zip(chip, steps)]
    return (x * SIDE + y) * SIDE + z


def fetch_kernel(
    own, slots, adj, feat, out,
    table, cols, req_out, req_in, counts, send, recv, total, marks,
    ask_send, ask_recv, row_send, row_recv,
):
    chip, rep, sign = place()
    barrier = pltpu.get_barrier_semaphore()

    @pl.loop(1, STORES)
    def _(i):
        pl.semaphore_signal(
            barrier, inc=1, device_id=(partner(i, chip, sign), rep), device_id_type=MESH
        )

    table[...] = jnp.zeros_like(table)
    upper = (iota((256, 256), 0) < iota((256, 256), 1)).astype(BF16)
    base = jnp.zeros((STORES, 1), F32)
    high = jnp.zeros((STORES, 128), F32)
    low = jnp.zeros((STORES, 128), F32)
    near_blocks = adj.shape[0] // 256
    for b in range(own.shape[1] // 256):
        span = slice(256 * b, 256 * b + 256)
        if b == near_blocks:
            base = jnp.zeros((STORES, 1), F32)
        owner = own[:, span]
        wanted = slots[:, span]
        jx = (sign * (chip[0] - (owner >> 4))) & 3
        jy = (sign * (chip[1] - ((owner >> 2) & 3))) & 3
        jz = (sign * (chip[2] - (owner & 3))) & 3
        slot = (((jx * 16) + jy * 4 + jz) * UNSTRIDE) & 63
        owned = (iota((STORES, 256), 0) == slot).astype(F32)
        owned_bf = owned.astype(BF16)
        before = dot(owned_bf, upper) + base
        base = base + jnp.sum(owned, axis=1, keepdims=True)
        position = jnp.sum(owned * before, axis=0, keepdims=True)
        if b >= near_blocks:
            position = position + CAP_NEAR
        slot_f = slot.astype(F32)
        for half in range(2):
            part = slice(128 * half, 128 * half + 128)
            table[2 * b + half : 2 * b + half + 1, 0:128] = slot_f[:, part]
            table[2 * b + half : 2 * b + half + 1, 128:256] = position[:, part]
        placed = (iota((128, 256), 0) == position.astype(jnp.int32)).astype(F32)
        high = high + dot_nt(owned_bf, (placed * (wanted >> 6).astype(F32)).astype(BF16))
        low = low + dot_nt(owned_bf, (placed * (wanted & 63).astype(F32)).astype(BF16))
    requests = (high * 64.0 + low).astype(jnp.int32)
    for i in range(STORES):
        req_out[i] = requests[i : i + 1, :]
    req_in[0] = requests[0:1, :]

    pl.semaphore_wait(barrier, STORES - 1)

    def ask(i):
        return pltpu.make_async_remote_copy(
            src_ref=req_out.at[i], dst_ref=req_in.at[i],
            send_sem=ask_send.at[i], recv_sem=ask_recv.at[i],
            device_id=(partner(i, chip, -sign), rep), device_id_type=MESH,
        )

    def give(i):
        return pltpu.make_async_remote_copy(
            src_ref=send.at[i], dst_ref=recv.at[i],
            send_sem=row_send.at[i], recv_sem=row_recv.at[i],
            device_id=(partner(i, chip, sign), rep), device_id_type=MESH,
        )

    @pl.loop(1, STORES)
    def _(i):
        ask(i).start()

    table_bf = table[...].astype(BF16)
    near_rows = adj.shape[0]
    for k in range(adj.shape[1]):
        entry = adj[:, k : k + 1]
        row_mark = (iota((near_rows, 32), 1) == (entry >> 7)).astype(F32).astype(BF16)
        found = dot(row_mark, table_bf)
        column = found[:, 0:128] * float(CAP) + found[:, 128:256]
        lane = iota((near_rows, 128), 1) == (entry & 127)
        cols[:, k : k + 1] = jnp.sum(jnp.where(lane, column, 0.0), axis=1, keepdims=True)

    @pl.loop(1, STORES)
    def _(i):
        ask(i).wait()

    asked = jnp.concatenate(
        [req_in[i].astype(F32) for i in range(STORES)] + [jnp.zeros((64, 128), F32)], axis=0
    )
    asked = jnp.transpose(asked)[0:CAP, :]
    total[0:CAP, 0:128] = asked

    nodes = feat.shape[0]

    @pl.loop(0, STORES // 4)
    def _(g):
        for m in range(4):
            i = g * 4 + m
            lane = iota((CAP, 128), 1) == i
            row = jnp.sum(jnp.where(lane, total[0:CAP, 0:128], 0.0), axis=1, keepdims=True)
            row = row.astype(jnp.int32)
            for c in range(nodes // 512):
                marks[CAP * m : CAP * m + CAP, 512 * c : 512 * c + 512] = (
                    (iota((CAP, 512), 1) + 512 * c == row).astype(F32).astype(BF16)
                )
        for h in range(3):
            span = slice(256 * h, 256 * h + 256)
            rows = dot(marks[...], feat[:, span]).astype(BF16)
            for m in range(4):
                send[g * 4 + m, :, span] = rows[CAP * m : CAP * m + CAP]
        for m in range(4):
            i = g * 4 + m

            @pl.when(i > 0)
            def _():
                give(i).start()

    recv[0] = send[0]

    groups, width = counts.shape[0], counts.shape[2]

    @pl.loop(0, near_rows // 32)
    def _(r):
        rows = pl.ds(pl.multiple_of(r * 32, 32), 32)
        mine = pl.ds(pl.multiple_of(near_rows + r * 32, 32), 32)
        picked = cols[rows, :]
        for c in range(groups):
            lane = (iota((32, width), 1) + width * c).astype(F32)
            tally = jnp.zeros((32, width), F32)
            for k in range(15):
                tally = tally + jnp.where(lane == picked[:, k : k + 1], 1.0, 0.0)
            counts[c, rows, :] = tally.astype(BF16)
            counts[c, mine, :] = jnp.where(lane == picked[:, 15:16], 1.0, 0.0).astype(BF16)

    total[...] = jnp.zeros_like(total)

    @pl.loop(0, groups)
    def _(c):
        for m in range(STORES // groups):
            i = c * (STORES // groups) + m

            @pl.when(i > 0)
            def _():
                give(i).wait_recv()

        block = recv[pl.ds(c * (STORES // groups), STORES // groups)].reshape(width, recv.shape[2])
        for h in range(3):
            span = slice(256 * h, 256 * h + 256)
            total[:, span] += dot(counts[c], block[:, span])

    features = recv.shape[2]
    out[:, 0:features] = total[near_rows : 2 * near_rows, :].astype(BF16)
    out[:, features : 2 * features] = (total[0:near_rows, :] / 15.0).astype(BF16)

    @pl.loop(1, STORES)
    def _(i):
        give(i).wait_send()


def fetch(owners, slots, adjacency, features):
    near = adjacency.shape[0]
    width = features.shape[1]
    groups = 8
    vmem = pl.BlockSpec(memory_space=pltpu.VMEM)
    return pl.pallas_call(
        fetch_kernel,
        out_shape=jax.ShapeDtypeStruct((near, 2 * width), BF16),
        in_specs=[vmem] * 4,
        out_specs=vmem,
        scratch_shapes=[
            pltpu.VMEM((32, 256), F32),
            pltpu.VMEM((near, 16), F32),
            pltpu.VMEM((STORES, 1, 128), jnp.int32),
            pltpu.VMEM((STORES, 1, 128), jnp.int32),
            pltpu.VMEM((groups, 2 * near, STORES // groups * CAP), BF16),
            pltpu.VMEM((STORES, CAP, width), BF16),
            pltpu.VMEM((STORES, CAP, width), BF16),
            pltpu.VMEM((2 * near, width), F32),
            pltpu.VMEM((4 * CAP, features.shape[0]), BF16),
            pltpu.SemaphoreType.DMA((STORES,)),
            pltpu.SemaphoreType.DMA((STORES,)),
            pltpu.SemaphoreType.DMA((STORES,)),
            pltpu.SemaphoreType.DMA((STORES,)),
        ],
        compiler_params=pltpu.CompilerParams(
            collective_id=0, has_side_effects=True, vmem_limit_bytes=58 << 20
        ),
    )(owners, slots, adjacency, features)


def spread_low():
    row, column = iota((384, 512), 0), iota((384, 512), 1)
    inner = column & 15
    return ((inner < 12) & (row == 12 * (column >> 4) + inner)).astype(F32).astype(BF16)


def spread_low_t():
    column, row = iota((512, 384), 1), iota((512, 384), 0)
    inner = row & 15
    return ((inner < 12) & (column == 12 * (row >> 4) + inner)).astype(F32).astype(BF16)


def spread_top(b):
    row, column = iota((256, 256), 0), iota((256, 256), 1)
    inner = column & 15
    return (
        ((inner >= 12) & (row == (column & -16) + 4 * (inner - 12) + b)).astype(F32).astype(BF16)
    )


def spread_top_t(b):
    column, row = iota((256, 256), 1), iota((256, 256), 0)
    inner = row & 15
    return (
        ((inner >= 12) & (column == (row & -16) + 4 * (inner - 12) + b)).astype(F32).astype(BF16)
    )


def gelu_parts(v):
    root = 0.7978845608028654
    square = v * v
    t = jnp.tanh(root * (v + 0.044715 * (v * square)))
    gate = 0.5 * (1.0 + t)
    slope = gate + 0.5 * v * (1.0 - t * t) * (root * (1.0 + 3.0 * 0.044715 * square))
    return v * gate, slope


def step_kernel(scale, x, wl, wt, at, at_t, lab, logits_out, grads, wtb, hidden, slope, dpre, left):
    classes = wt.shape[1]
    width = wl.shape[1]
    seeds = at.shape[0]
    near = x.shape[0]
    wtb[...] = jnp.zeros_like(wtb)
    wtb[:, 0:classes] = wt[...].astype(BF16)
    for n in range(width // 256):
        span = slice(256 * n, 256 * n + 256)
        value, rise = gelu_parts(dot(x[...], wl[:, span].astype(BF16)))
        hidden[:, span] = value.astype(BF16)
        slope[:, span] = rise
    fan = at.shape[1]
    picks = jnp.zeros((seeds, near), F32)
    picks_t = jnp.zeros((near, seeds), F32)
    for k in range(fan):
        picks = picks + (iota((seeds, near), 1) == at[:, k : k + 1]).astype(F32)
        picks_t = picks_t + (iota((near, seeds), 0) == at_t[k : k + 1, :]).astype(F32)
    picks = picks.astype(BF16)
    picks_t = picks_t.astype(BF16)
    mean = (dot(picks, hidden[...]) / float(fan)).astype(BF16)
    own = hidden[0:seeds, :]
    logits = dot(own, wtb[0:width, :]) + dot(mean, wtb[width : 2 * width, :])
    logits_out[...] = logits[:, 0:classes]
    lane = iota(logits.shape, 1)
    powers = jnp.where(lane < classes, jnp.exp(logits), 0.0)
    chances = powers / jnp.sum(powers, axis=1, keepdims=True)
    targets = (lane == lab[...]).astype(F32)
    dlogits = ((chances - targets) * scale).astype(BF16)
    first = dot_nt(dlogits, wtb[0:width, :])
    second = dot_nt(dlogits, wtb[width : 2 * width, :]) / float(fan)
    second_high = second.astype(BF16)
    second_low = (second - second_high.astype(F32)).astype(BF16)
    for n in range(width // 256):
        span = slice(256 * n, 256 * n + 256)
        back = dot(picks_t, second_high[:, span]) + dot(picks_t, second_low[:, span])
        dpre[seeds:near, span] = (back[seeds:near] * slope[seeds:near, span]).astype(BF16)
        dpre[0:seeds, span] = ((back[0:seeds] + first[:, span]) * slope[0:seeds, span]).astype(BF16)
    low_t = spread_low_t()
    for m in range(x.shape[1] // 384):
        left[512 * m : 512 * m + 512, :] = dot_nt(low_t, x[:, 384 * m : 384 * m + 384]).astype(BF16)
    for b in range(width // 256):
        span = slice(256 * b, 256 * b + 256)
        top_t = spread_top_t(b)
        for m in range(2 * width // 256):
            source = own if m < width // 256 else mean
            at_col = 256 * (m % (width // 256))
            top_left = dot_nt(top_t, source[:, at_col : at_col + 256]).astype(BF16)
            rows = slice(256 * m, 256 * m + 256)
            grads[rows, span] = (dot(left[rows, :], dpre[:, span]) + dot(top_left, dlogits)).astype(BF16)


def local_step(x, weights_low, weights_top, adjacency_top, labels, scale):
    near = x.shape[0]
    seeds, fan = adjacency_top.shape
    width = weights_low.shape[1]
    vmem = pl.BlockSpec(memory_space=pltpu.VMEM)
    return pl.pallas_call(
        functools.partial(step_kernel, scale),
        out_shape=(
            jax.ShapeDtypeStruct((seeds, weights_top.shape[1]), F32),
            jax.ShapeDtypeStruct((2 * width, width), BF16),
        ),
        in_specs=[vmem] * 6,
        out_specs=(vmem, vmem),
        scratch_shapes=[
            pltpu.VMEM((2 * width, 256), BF16),
            pltpu.VMEM((near, width), BF16),
            pltpu.VMEM((near, width), F32),
            pltpu.VMEM((near, width), BF16),
            pltpu.VMEM((2 * width, near), BF16),
        ],
        compiler_params=pltpu.CompilerParams(vmem_limit_bytes=48 << 20),
    )(x, weights_low, weights_top, adjacency_top, adjacency_top.T, labels[:, None])


def adam_parts(moment, square, gradient):
    moment_new = beta_one * moment + (1.0 - beta_one) * gradient
    square_new = beta_two * square + (1.0 - beta_two) * gradient * gradient
    update = moment_new / bias_one / (jnp.sqrt(square_new / bias_two) + adam_eps)
    return learn_rate * update, moment_new, square_new


def reduce_kernel(
    grads, ml, vl, mt, vt, everyone, ml_out, vl_out, mt_out, vt_out,
    pair, halves, parts, share, top, pair_send, pair_recv, part_send, part_recv,
    all_send, all_recv, twin_send, twin_recv,
):
    chip, rep, sign = place()
    me = lax.axis_index("store")
    other = 1 - rep
    classes = mt.shape[1]
    barrier = pltpu.get_barrier_semaphore()

    @pl.loop(1, STORES)
    def _(i):
        pl.semaphore_signal(
            barrier, inc=1, device_id=(partner(i, chip, sign), rep), device_id_type=MESH
        )

    pl.semaphore_signal(barrier, inc=1, device_id=(me, other), device_id_type=MESH)
    pl.semaphore_wait(barrier, STORES)

    swap = pltpu.make_async_remote_copy(
        src_ref=grads.at[:, other], dst_ref=pair, send_sem=pair_send, recv_sem=pair_recv,
        device_id=(me, other), device_id_type=MESH,
    )
    swap.start()
    swap.wait()

    def hand(i):
        return pltpu.make_async_remote_copy(
            src_ref=halves.at[i], dst_ref=parts.at[i],
            send_sem=part_send.at[i], recv_sem=part_recv.at[i],
            device_id=(partner(i, chip, sign), rep), device_id_type=MESH,
        )

    @pl.loop(0, STORES)
    def _(i):
        to = partner(i, chip, sign)
        halves[i] = (grads[to, rep].astype(F32) + pair[to].astype(F32)).astype(BF16)

        @pl.when(i > 0)
        def _():
            hand(i).start()

    def add(i, so_far):
        hand(i).wait_recv()
        return so_far + parts[i].astype(F32)

    gradient = lax.fori_loop(1, STORES, add, halves[0].astype(F32))

    step, moment, square = adam_parts(ml[...], vl[...], gradient[0:12, :])
    ml_out[...] = moment
    vl_out[...] = square
    share[0:12, :] = step
    for a in range(4):
        for b in range(4):
            top[4 * a + b : 4 * a + b + 1, :] = gradient[12 + a : 13 + a, 256 * b : 256 * b + 256]
    step, moment, square = adam_parts(mt[...], vt[...], top[:, 0:classes])
    mt_out[...] = moment
    vt_out[...] = square
    top[:, 0:classes] = step
    for a in range(4):
        for b in range(4):
            share[12 + a : 13 + a, 256 * b : 256 * b + 256] = top[4 * a + b : 4 * a + b + 1, :]
    everyone[me, rep] = share[...].astype(BF16)

    def tell(i):
        return pltpu.make_async_remote_copy(
            src_ref=everyone.at[me, rep], dst_ref=everyone.at[me, rep],
            send_sem=all_send.at[i], recv_sem=all_recv.at[i],
            device_id=(partner(i, chip, sign), rep), device_id_type=MESH,
        )

    def twin(i):
        came = partner(i, chip, -sign)
        return pltpu.make_async_remote_copy(
            src_ref=everyone.at[came, rep], dst_ref=everyone.at[came, rep],
            send_sem=twin_send.at[i], recv_sem=twin_recv.at[i],
            device_id=(me, other), device_id_type=MESH,
        )

    @pl.loop(1, STORES)
    def _(i):
        tell(i).start()

    twin(0).start()

    @pl.loop(1, STORES)
    def _(i):
        tell(i).wait_recv()
        twin(i).start()

    @pl.loop(0, STORES)
    def _(i):
        twin(i).wait()

        @pl.when(i > 0)
        def _():
            tell(i).wait_send()
            hand(i).wait_send()


def reduce_and_update(grads, first_low, second_low, first_top, second_top):
    tile = grads.shape[2:]
    vmem = pl.BlockSpec(memory_space=pltpu.VMEM)
    low = jax.ShapeDtypeStruct(first_low.shape, F32)
    top = jax.ShapeDtypeStruct(first_top.shape, F32)
    many = pltpu.SemaphoreType.DMA((STORES,))
    return pl.pallas_call(
        reduce_kernel,
        out_shape=(jax.ShapeDtypeStruct(grads.shape, BF16), low, low, top, top),
        in_specs=[vmem] * 5,
        out_specs=(vmem,) * 5,
        scratch_shapes=[
            pltpu.VMEM((STORES,) + tile, BF16),
            pltpu.VMEM((STORES,) + tile, BF16),
            pltpu.VMEM((STORES,) + tile, BF16),
            pltpu.VMEM(tile, F32),
            pltpu.VMEM((16, 256), F32),
            pltpu.SemaphoreType.DMA,
            pltpu.SemaphoreType.DMA,
            many, many, many, many, many, many,
        ],
        compiler_params=pltpu.CompilerParams(
            collective_id=1, has_side_effects=True, vmem_limit_bytes=32 << 20
        ),
    )(grads, first_low, second_low, first_top, second_top)


def finish_kernel(steps, wl, wt, wl_out, wt_out):
    wl_out[...] = wl[...] - dot(spread_low(), steps[...])
    classes = wt.shape[1]
    for m in range(2):
        rows = slice(256 * m, 256 * m + 256)
        top = jnp.zeros((256, 256), F32)
        for b in range(4):
            top = top + dot(spread_top(b), steps[rows, 256 * b : 256 * b + 256])
        wt_out[rows, :] = wt[rows, :] - top[:, 0:classes]


def finish(steps, weights_low, weights_top):
    rows, width = weights_low.shape
    tops, classes = weights_top.shape
    low = pl.BlockSpec((384, width), lambda i: (i, 0))
    top = pl.BlockSpec((512, classes), lambda i: (i, 0))
    return pl.pallas_call(
        finish_kernel,
        grid=(4,),
        out_shape=(
            jax.ShapeDtypeStruct((rows, width), F32),
            jax.ShapeDtypeStruct((tops, classes), F32),
        ),
        in_specs=[pl.BlockSpec((512, width), lambda i: (i, 0)), low, top],
        out_specs=(low, top),
        compiler_params=pltpu.CompilerParams(vmem_limit_bytes=32 << 20),
    )(steps, weights_low, weights_top)


def per_device(
    features,
    owners_near,
    slots_near,
    owners_far,
    slots_far,
    adjacency_low,
    adjacency_top,
    labels,
    weights_low,
    weights_top,
    first_low,
    second_low,
    first_top,
    second_top,
):
    near = adjacency_low.shape[0]
    owners = jnp.concatenate([owners_near[:, 0], owners_far[:, 0]])[None, :]
    slots = jnp.concatenate([slots_near[:, 0], slots_far[:, 0]])[None, :]
    entries = jnp.concatenate([adjacency_low, jnp.arange(near, dtype=jnp.int32)[:, None]], axis=1)
    x = fetch(owners, slots, entries, features)
    members = lax.axis_size(("store", "rep"))
    scale = 1.0 / (labels.shape[0] * members)
    logits, grads = local_step(x, weights_low, weights_top, adjacency_top, labels, scale)
    grads = grads.reshape(STORES, 2, 16, grads.shape[1])
    steps, new_first_low, new_second_low, new_first_top, new_second_top = reduce_and_update(
        grads, first_low, second_low, first_top, second_top
    )
    new_low, new_top = finish(steps.reshape(-1, grads.shape[3]), weights_low, weights_top)
    return (logits, new_low, new_first_low, new_second_low, new_top, new_first_top, new_second_top)


def solution(mesh):
    both = P(("store", "rep"), None)
    return jax.shard_map(
        per_device,
        mesh=mesh,
        in_specs=(
            P("store", None), both, both, both, both, both, both, P(("store", "rep")),
            P(), P(), both, both, both, both,
        ),
        out_specs=(both, P(), both, both, P(), both, both),
        check_vma=False,
    )
```

time: 892 us -> 278 us (0.31); the launches traced: 880 us -> 278 us
  waiting for transfers between devices: 427 us -> 0 us
  local copies, waits for them, and re-layouts: 285 us -> 18.2 us
  Pallas kernels: 0 us -> 256 us
  other arithmetic: 97 us -> 2.29 us
  starting transfers between devices: 39.4 us -> 0 us
  matrix products: 16.4 us -> 0 us
  between operations: 14.4 us -> 0.73 us
    pallas_call x0 -> x4, Pallas kernels: none -> 256 us  [the longest x1 168 us: fetch(): pl.pallas_call(fetch_kernel, out_shape=jax.ShapeDtypeStruct((near, 2 * wi...]
    gather x29 -> x0, local copies, waits for them, and re-layouts: 206 us -> none  [the longest x15 93.8 us: local_step(): gathered = gathered + fetched[adjacency_low[:, column]].astype(jnp.float32)]
    psum x1 -> x0, waiting for transfers between devices: 173 us -> none  [per_device(): whole_low, whole_top = lax.psum((grad_low, grad_top), ('store', 'rep'))]
    all_gather x2 -> x0, waiting for transfers between devices: 134 us -> none  [the longest x1 68.9 us: per_device(): lax.all_gather(part_low, ('store', 'rep'), axis=0, tiled=True)]
    all_to_all x4 -> x0, waiting for transfers between devices: 120 us -> none  [the longest x2 117 us: fetch_rows(): lax.all_to_all(found, 'store', split_axis=0, concat_axis=0, tiled=True)]
    scatter-add x10 -> x0, other arithmetic: 45 us -> none  [local_step(): dhidden = dhidden.at[adjacency_top[:, column]].add(spread)]
    scatter x1 -> x0, local copies, waits for them, and re-layouts: 42.9 us -> none  [bucket(): jnp.zeros((stores, capacity), jnp.int32).at[owners, places].set(slots)]
    all_to_all x4 -> x0, starting transfers between devices: 38.8 us -> none  [the longest x2 21.7 us: fetch_rows(): lax.all_to_all(requests, 'store', split_axis=0, concat_axis=0, tiled=True)]
  transfers between devices with their start and end apart: 7 -> 0, of which waited for: 5 -> 0; matrix products, arithmetic and copies ran while one was open for 11% -> 0% of each run, Pallas kernels for 0% -> 0%
where the time goes in v1:
time: 278 us
  Pallas kernels  256 us (92%)
  local copies, waits for them, and re-layouts  18.2 us (7%)
    pallas_call x1, Pallas kernels, fetch(): pl.pallas_call(fetch_kernel, out_shape=jax.ShapeDtypeStruct((near, 2 * wi...  168 us
    pallas_call x1, Pallas kernels, reduce_and_update(): pl.pallas_call(reduce_kernel, out_shape=(jax.ShapeDtypeStruct(grads.shape...  69.1 us
    unnamed x28, local copies, waits for them, and re-layouts  15.4 us
    pallas_call x1, Pallas kernels, local_step(): pl.pallas_call(functools.partial(step_kernel, scale), out_shape=(jax.Shap...  15.3 us

profile of v1, /device:TPU:1, one launch (start us, length us, event | category | flops | bytes accessed | tf_op | source)
XLA Modules:
  0.0 277.6 jit_solution(8238582187262339464)
XLA Ops:
  0.6 0.0 copy-start.9
  0.7 0.8 pad_add_fusion.1
  1.5 0.6 broadcast_in_dim.10.own
  2.1 0.7 pad_add_fusion.2
  2.8 0.6 broadcast_in_dim.11.slots
  3.4 0.8 pad_add_fusion
  4.2 0.8 copy.31.lab
  4.9 0.8 copy.30.at
  5.7 0.8 copy.28.adj
  6.6 0.0 copy-start.6
  6.6 167.7 %shard_map.189.x = bf16[512,1536]{1,0:T(8,128)(2,1)} custom-call(s32[1,3584]{1,0:T(1,128)} %broadcast_in_dim.10.own, s32[1,3584]{1,0:T(1,128)} %broadcast_in_dim.11.slots, s32[512,16]{1,0:T(8,128)} %copy.28.adj, bf16[2048,768]{1,0:T(8,128)(2,1)} %feat.1), custom_call_target="tpu_custom_call" | custom-call | tf_op jit(solution)/shard_map/pallas_call | solution.py:215
  174.2 0.0 copy-done.9
  174.2 1.0 copy.29.wt
  175.2 0.0 copy-done.6
  175.3 0.0 copy-start.1
  175.3 1.4 copy-done.1
  176.7 0.0 copy-start.4
  176.7 0.0 copy-start.5
  176.7 0.0 copy-start.7
  176.7 0.0 copy-start.8
  176.7 15.3 %shard_map.190 = (f32[128,153]{1,0:T(8,128)S(1)}, bf16[2048,1024]{1,0:T(8,128)(2,1)}) custom-call(bf16[512,1536]{1,0:T(8,128)(2,1)S(1)} %copy-done.1, f32[1536,1024]{1,0:T(8,128)} %wl.3, f32[2048,153]{1,0:T(8,128)S(1)} %copy.29.wt, s32[128,10]{1,0:T(8,128)S(1)} %copy.30.at, s32[10,128]{1,0:T(8,128)S(1)} %bitcast.10, s32[128,1]{1,0:T(8,128)S(1)} %copy.31.lab), custom_call_target="tpu_custom_call" | custom-call | tf_op jit(solution)/shard_map/pallas_call | solution.py:335
  192.0 0.7 copy.33
  192.7 0.0 copy-done.4
  192.7 0.0 copy-done.5
  192.7 0.0 copy-done.7
  192.7 0.0 copy-done.8
  192.7 0.0 copy-start.2
  192.7 2.2 copy-done.2
  194.9 69.1 %shard_map.191 = (bf16[64,2,16,1024]{3,2,1,0:T(8,128)(2,1)S(1)}, f32[12,1024]{1,0:T(8,128)S(1)}, f32[12,1024]{1,0:T(8,128)S(1)}, f32[16,153]{1,0:T(8,128)S(1)}, f32[16,153]{1,0:T(8,128)S(1)}) custom-call(bf16[64,2,16,1024]{3,2,1,0:T(8,128)(2,1)S(1)} %bitcast.9, f32[12,1024]{1,0:T(8,128)S(1)} %copy-done.4, f32[12,1024]{1,0:T(8,128)S(1)} %copy-done.5, ...), custom_call_target="tpu_custom_call" | custom-call | tf_op jit(solution)/shard_map/pallas_call | solution.py:468
  264.1 0.0 copy-start
  264.1 2.8 copy-done
  266.8 4.3 %shard_map.192 = (f32[1536,1024]{1,0:T(8,128)}, f32[2048,153]{1,0:T(8,128)S(1)}) custom-call(bf16[2048,1024]{1,0:T(8,128)(2,1)S(1)} %bitcast.8, f32[1536,1024]{1,0:T(8,128)S(1)} %copy-done, f32[2048,153]{1,0:T(8,128)S(1)} %copy.29.wt), custom_call_target="tpu_custom_call" | custom-call | tf_op jit(solution)/shard_map/pallas_call | solution.py:505
  271.1 0.0 copy-start.3
  271.1 1.3 copy-done.3
  272.5 2.7 copy.34
  275.2 0.6 copy.39
  275.8 0.6 copy.40
  276.4 0.6 copy.41
  277.0 0.6 copy.42
  (1 shorter events, 0.0 us)
Async XLA Ops:
  0.6 173.6 %copy-start.9 = (f32[2048,153]{0,1:T(8,128)S(1)}, f32[2048,153]{0,1:T(8,128)}, u32[]{:S(2)}) copy-start(f32[2048,153]{0,1:T(8,128)} %param.23) | copy-start | bytes 3760132
  6.6 168.7 %copy-start.6 = (s32[128,10]{0,1:T(8,128)S(1)}, s32[128,10]{0,1:T(8,128)}, u32[]{:S(2)}) copy-start(s32[128,10]{0,1:T(8,128)} %param.20) | copy-start | bytes 15364
  175.3 1.4 copy-start.1
  176.7 16.0 %copy-start.4 = (f32[12,1024]{1,0:T(8,128)S(1)}, f32[12,1024]{1,0:T(8,128)}, u32[]{:S(2)}) copy-start(f32[12,1024]{1,0:T(8,128)} %ml.1) | copy-start | bytes 147460
  176.7 16.0 %copy-start.5 = (f32[12,1024]{1,0:T(8,128)S(1)}, f32[12,1024]{1,0:T(8,128)}, u32[]{:S(2)}) copy-start(f32[12,1024]{1,0:T(8,128)} %vl.1) | copy-start | bytes 147460
  176.7 16.0 %copy-start.7 = (f32[16,153]{1,0:T(8,128)S(1)}, f32[16,153]{1,0:T(8,128)}, u32[]{:S(2)}) copy-start(f32[16,153]{1,0:T(8,128)} %mt.1) | copy-start | bytes 29380
  176.7 16.0 %copy-start.8 = (f32[16,153]{1,0:T(8,128)S(1)}, f32[16,153]{1,0:T(8,128)}, u32[]{:S(2)}) copy-start(f32[16,153]{1,0:T(8,128)} %vt.1) | copy-start | bytes 29380
  192.7 2.2 copy-start.2
  264.1 2.8 %copy-start = (f32[1536,1024]{1,0:T(8,128)S(1)}, f32[1536,1024]{1,0:T(8,128)}, u32[]{:S(2)}) copy-start(f32[1536,1024]{1,0:T(8,128)} %wl.3) | copy-start | bytes 18874372
  271.1 1.3 copy-start.3

commit v2 on v1

--- a/solution.py
+++ b/solution.py
@@ -275,7 +275,7 @@
     return v * gate, slope
 
 
-def step_kernel(scale, x, wl, wt, at, at_t, lab, logits_out, grads, wtb, hidden, slope, dpre, left):
+def step_part(scale, x, wl, wt, at, at_t, lab, logits_out, grads, wtb, hidden, slope, dpre, left):
     classes = wt.shape[1]
     width = wl.shape[1]
     seeds = at.shape[0]
@@ -324,31 +324,10 @@
             at_col = 256 * (m % (width // 256))
             top_left = dot_nt(top_t, source[:, at_col : at_col + 256]).astype(BF16)
             rows = slice(256 * m, 256 * m + 256)
-            grads[rows, span] = (dot(left[rows, :], dpre[:, span]) + dot(top_left, dlogits)).astype(BF16)
-
-
-def local_step(x, weights_low, weights_top, adjacency_top, labels, scale):
-    near = x.shape[0]
-    seeds, fan = adjacency_top.shape
-    width = weights_low.shape[1]
-    vmem = pl.BlockSpec(memory_space=pltpu.VMEM)
-    return pl.pallas_call(
-        functools.partial(step_kernel, scale),
-        out_shape=(
-            jax.ShapeDtypeStruct((seeds, weights_top.shape[1]), F32),
-            jax.ShapeDtypeStruct((2 * width, width), BF16),
-        ),
-        in_specs=[vmem] * 6,
-        out_specs=(vmem, vmem),
-        scratch_shapes=[
-            pltpu.VMEM((2 * width, 256), BF16),
-            pltpu.VMEM((near, width), BF16),
-            pltpu.VMEM((near, width), F32),
-            pltpu.VMEM((near, width), BF16),
-            pltpu.VMEM((2 * width, near), BF16),
-        ],
-        compiler_params=pltpu.CompilerParams(vmem_limit_bytes=48 << 20),
-    )(x, weights_low, weights_top, adjacency_top, adjacency_top.T, labels[:, None])
+            block = dot(left[rows, :], dpre[:, span]) + dot(top_left, dlogits)
+            grads[m // 2, 2 * (m % 2) : 2 * (m % 2) + 2, :, :, :, span] = block.astype(BF16).reshape(
+                2, SIDE, 2, 16, 256
+            )
 
 
 def adam_parts(moment, square, gradient):
@@ -358,62 +337,125 @@
     return learn_rate * update, moment_new, square_new
 
 
-def reduce_kernel(
-    grads, ml, vl, mt, vt, everyone, ml_out, vl_out, mt_out, vt_out,
-    pair, halves, parts, share, top, pair_send, pair_recv, part_send, part_recv,
-    all_send, all_recv, twin_send, twin_recv,
+SPANS = (slice(0, 384), slice(384, 768), slice(768, 1024))
+
+
+def block_of(axes, fixed, tail):
+    return tuple(fixed.get(axis, slice(None)) for axis in axes) + tail
+
+
+def reduce_part(
+    chip, rep, grads, ml, vl, mt, vt, everyone, ml_out, vl_out, mt_out, vt_out,
+    pair, halves, got_one, sum_one, got_two, sum_two, got_three, share, top,
+    pair_send, pair_recv, down_send, down_recv, up_send, up_recv, twin_send, twin_recv,
 ):
-    chip, rep, sign = place()
-    me = lax.axis_index("store")
     other = 1 - rep
     classes = mt.shape[1]
-    barrier = pltpu.get_barrier_semaphore()
-
-    @pl.loop(1, STORES)
-    def _(i):
-        pl.semaphore_signal(
-            barrier, inc=1, device_id=(partner(i, chip, sign), rep), device_id_type=MESH
+    every = slice(None)
+
+    def copy(src, dst, send_sem, recv_sem, at, core):
+        return pltpu.make_async_remote_copy(
+            src_ref=src, dst_ref=dst, send_sem=send_sem, recv_sem=recv_sem,
+            device_id=((at[0] * SIDE + at[1]) * SIDE + at[2], core), device_id_type=MESH,
         )
 
-    pl.semaphore_signal(barrier, inc=1, device_id=(me, other), device_id_type=MESH)
-    pl.semaphore_wait(barrier, STORES)
-
-    swap = pltpu.make_async_remote_copy(
-        src_ref=grads.at[:, other], dst_ref=pair, send_sem=pair_send, recv_sem=pair_recv,
-        device_id=(me, other), device_id_type=MESH,
-    )
-    swap.start()
-    swap.wait()
-
-    def hand(i):
-        return pltpu.make_async_remote_copy(
-            src_ref=halves.at[i], dst_ref=parts.at[i],
-            send_sem=part_send.at[i], recv_sem=part_recv.at[i],
-            device_id=(partner(i, chip, sign), rep), device_id_type=MESH,
-        )
-
-    @pl.loop(0, STORES)
-    def _(i):
-        to = partner(i, chip, sign)
-        halves[i] = (grads[to, rep].astype(F32) + pair[to].astype(F32)).astype(BF16)
-
-        @pl.when(i > 0)
-        def _():
-            hand(i).start()
-
-    def add(i, so_far):
-        hand(i).wait_recv()
-        return so_far + parts[i].astype(F32)
-
-    gradient = lax.fori_loop(1, STORES, add, halves[0].astype(F32))
-
-    step, moment, square = adam_parts(ml[...], vl[...], gradient[0:12, :])
+    def moved(axis, step):
+        return [lax.rem(c + step, SIDE) if n == axis else c for n, c in enumerate(chip)]
+
+    swaps = []
+    for c, span in enumerate(SPANS):
+        swaps.append(copy(
+            grads.at[:, :, :, other, :, span], pair.at[:, :, :, :, span],
+            pair_send.at[c], pair_recv.at[c], chip, other,
+        ))
+        swaps[c].start()
+    sent = list(swaps)
+    got = (got_one, got_two, got_three)
+    waiting = []
+    for c, span in enumerate(SPANS):
+        swaps[c].wait_recv()
+
+        @pl.loop(0, SIDE)
+        def _(x):
+            for y in range(SIDE):
+                for z in range(SIDE):
+                    halves[x, y, z, :, span] = (
+                        grads[x, y, z, rep, :, span].astype(F32) + pair[x, y, z, :, span].astype(F32)
+                    ).astype(BF16)
+
+        axes, first = (0, 1, 2), c
+        copies = []
+        for k in range(1, SIDE):
+            to = moved(first, k)
+            copies.append(copy(
+                halves.at[block_of(axes, {first: to[first]}, (every, span))],
+                got_one.at[k - 1, :, :, :, span],
+                down_send.at[0, c, k - 1], down_recv.at[0, c, k - 1], to, rep,
+            ))
+            copies[-1].start()
+        sent += copies
+        waiting.append(copies)
+    following = []
+    for c, span in enumerate(SPANS):
+        first, second = c, (c + 1) % 3
+        left = tuple(n for n in range(3) if n != first)
+        for made in waiting[c]:
+            made.wait_recv()
+        for a in range(SIDE):
+            for b in range(SIDE):
+                spot = {left[0]: a, left[1]: b, first: chip[first]}
+                total = halves[block_of((0, 1, 2), spot, (every, span))].astype(F32)
+                for k in range(1, SIDE):
+                    total = total + got_one[k - 1, a, b, :, span].astype(F32)
+                sum_one[a, b, :, span] = total.astype(BF16)
+        copies = []
+        for k in range(1, SIDE):
+            to = moved(second, k)
+            copies.append(copy(
+                sum_one.at[block_of(left, {second: to[second]}, (every, span))],
+                got_two.at[k - 1, :, :, span],
+                down_send.at[1, c, k - 1], down_recv.at[1, c, k - 1], to, rep,
+            ))
+            copies[-1].start()
+        sent += copies
+        following.append(copies)
+    waiting, following = following, []
+    for c, span in enumerate(SPANS):
+        first, second, third = c, (c + 1) % 3, (c + 2) % 3
+        left = tuple(n for n in range(3) if n != first)
+        for made in waiting[c]:
+            made.wait_recv()
+        for a in range(SIDE):
+            spot = {third: a, second: chip[second]}
+            total = sum_one[block_of(left, spot, (every, span))].astype(F32)
+            for k in range(1, SIDE):
+                total = total + got_two[k - 1, a, :, span].astype(F32)
+            sum_two[a, :, span] = total.astype(BF16)
+        copies = []
+        for k in range(1, SIDE):
+            to = moved(third, k)
+            copies.append(copy(
+                sum_two.at[to[third], :, span], got_three.at[k - 1, :, span],
+                down_send.at[2, c, k - 1], down_recv.at[2, c, k - 1], to, rep,
+            ))
+            copies[-1].start()
+        sent += copies
+        following.append(copies)
+    for c, span in enumerate(SPANS):
+        for made in following[c]:
+            made.wait_recv()
+        total = sum_two[chip[(c + 2) % 3], :, span].astype(F32)
+        for k in range(1, SIDE):
+            total = total + got_three[k - 1, :, span].astype(F32)
+        share[:, span] = total
+
+    step, moment, square = adam_parts(ml[...], vl[...], share[0:12, :])
     ml_out[...] = moment
     vl_out[...] = square
-    share[0:12, :] = step
     for a in range(4):
         for b in range(4):
-            top[4 * a + b : 4 * a + b + 1, :] = gradient[12 + a : 13 + a, 256 * b : 256 * b + 256]
+            top[4 * a + b : 4 * a + b + 1, :] = share[12 + a : 13 + a, 256 * b : 256 * b + 256]
+    share[0:12, :] = step
     step, moment, square = adam_parts(mt[...], vt[...], top[:, 0:classes])
     mt_out[...] = moment
     vt_out[...] = square
@@ -421,69 +463,110 @@
     for a in range(4):
         for b in range(4):
             share[12 + a : 13 + a, 256 * b : 256 * b + 256] = top[4 * a + b : 4 * a + b + 1, :]
-    everyone[me, rep] = share[...].astype(BF16)
-
-    def tell(i):
-        return pltpu.make_async_remote_copy(
-            src_ref=everyone.at[me, rep], dst_ref=everyone.at[me, rep],
-            send_sem=all_send.at[i], recv_sem=all_recv.at[i],
-            device_id=(partner(i, chip, sign), rep), device_id_type=MESH,
-        )
-
-    def twin(i):
-        came = partner(i, chip, -sign)
-        return pltpu.make_async_remote_copy(
-            src_ref=everyone.at[came, rep], dst_ref=everyone.at[came, rep],
-            send_sem=twin_send.at[i], recv_sem=twin_recv.at[i],
-            device_id=(me, other), device_id_type=MESH,
-        )
-
-    @pl.loop(1, STORES)
-    def _(i):
-        tell(i).start()
-
-    twin(0).start()
-
-    @pl.loop(1, STORES)
-    def _(i):
-        tell(i).wait_recv()
-        twin(i).start()
-
-    @pl.loop(0, STORES)
-    def _(i):
-        twin(i).wait()
-
-        @pl.when(i > 0)
-        def _():
-            tell(i).wait_send()
-            hand(i).wait_send()
-
-
-def reduce_and_update(grads, first_low, second_low, first_top, second_top):
-    tile = grads.shape[2:]
+    everyone[chip[0], chip[1], chip[2], rep] = share[...].astype(BF16)
+
+    waiting = [[] for span in SPANS]
+    twins = []
+    for level in range(4):
+        for c, span in enumerate(SPANS):
+            order = ((c + 2) % 3, (c + 1) % 3, c)
+            for made in waiting[c]:
+                made.wait_recv()
+            if level < 3:
+                spot = {n: chip[n] for n in order[level:]}
+                block = everyone.at[block_of((0, 1, 2), spot, (rep, every, span))]
+                waiting[c] = []
+                for k in range(1, SIDE):
+                    waiting[c].append(copy(
+                        block, block, up_send.at[level, c, k - 1], up_recv.at[level, c, k - 1],
+                        moved(order[level], k), rep,
+                    ))
+                    waiting[c][-1].start()
+                sent += waiting[c]
+            if level >= 2:
+                for k in range(1 if level == 3 else 0, SIDE if level == 3 else 1):
+                    spot = {c: lax.rem(chip[c] + SIDE - k, SIDE)}
+                    block = everyone.at[block_of((0, 1, 2), spot, (rep, every, span))]
+                    twins.append(copy(
+                        block, block, twin_send.at[c, k], twin_recv.at[c, k], chip, other
+                    ))
+                    twins[-1].start()
+    for made in twins:
+        made.wait()
+    for made in sent:
+        made.wait_send()
+
+
+def train_kernel(
+    scale, x, wl, wt, at, at_t, lab, ml, vl, mt, vt,
+    logits_out, everyone, ml_out, vl_out, mt_out, vt_out,
+    wtb, hidden, slope, dpre, left, grads, *scratch,
+):
+    chip, rep, _ = place()
+    barrier = pltpu.get_barrier_semaphore()
+    for axis in range(3):
+        for k in range(1, SIDE):
+            at_k = [lax.rem(c + k, SIDE) if n == axis else c for n, c in enumerate(chip)]
+            to = (at_k[0] * SIDE + at_k[1]) * SIDE + at_k[2]
+            pl.semaphore_signal(barrier, inc=1, device_id=(to, rep), device_id_type=MESH)
+    pl.semaphore_signal(
+        barrier, inc=1, device_id=(lax.axis_index("store"), 1 - rep), device_id_type=MESH
+    )
+    step_part(scale, x, wl, wt, at, at_t, lab, logits_out, grads, wtb, hidden, slope, dpre, left)
+    pl.semaphore_wait(barrier, 10)
+    reduce_part(
+        chip, rep, grads, ml, vl, mt, vt, everyone, ml_out, vl_out, mt_out, vt_out, *scratch
+    )
+
+
+def train(x, weights_low, weights_top, adjacency_top, labels, scale, ml, vl, mt, vt):
+    near = x.shape[0]
+    seeds, fan = adjacency_top.shape
+    width = weights_low.shape[1]
+    cube = (SIDE, SIDE, SIDE)
+    tile = (16, width)
     vmem = pl.BlockSpec(memory_space=pltpu.VMEM)
-    low = jax.ShapeDtypeStruct(first_low.shape, F32)
-    top = jax.ShapeDtypeStruct(first_top.shape, F32)
-    many = pltpu.SemaphoreType.DMA((STORES,))
+    low = jax.ShapeDtypeStruct(ml.shape, F32)
+    top = jax.ShapeDtypeStruct(mt.shape, F32)
+    hops = pltpu.SemaphoreType.DMA((3, 3, 3))
     return pl.pallas_call(
-        reduce_kernel,
-        out_shape=(jax.ShapeDtypeStruct(grads.shape, BF16), low, low, top, top),
-        in_specs=[vmem] * 5,
-        out_specs=(vmem,) * 5,
+        functools.partial(train_kernel, scale),
+        out_shape=(
+            jax.ShapeDtypeStruct((seeds, weights_top.shape[1]), F32),
+            jax.ShapeDtypeStruct(cube + (2,) + tile, BF16),
+            low, low, top, top,
+        ),
+        in_specs=[vmem] * 10,
+        out_specs=(vmem,) * 6,
         scratch_shapes=[
-            pltpu.VMEM((STORES,) + tile, BF16),
-            pltpu.VMEM((STORES,) + tile, BF16),
-            pltpu.VMEM((STORES,) + tile, BF16),
+            pltpu.VMEM((2 * width, 256), BF16),
+            pltpu.VMEM((near, width), BF16),
+            pltpu.VMEM((near, width), F32),
+            pltpu.VMEM((near, width), BF16),
+            pltpu.VMEM((2 * width, near), BF16),
+            pltpu.VMEM(cube + (2,) + tile, BF16),
+            pltpu.VMEM(cube + tile, BF16),
+            pltpu.VMEM(cube + tile, BF16),
+            pltpu.VMEM((SIDE - 1, SIDE, SIDE) + tile, BF16),
+            pltpu.VMEM((SIDE, SIDE) + tile, BF16),
+            pltpu.VMEM((SIDE - 1, SIDE) + tile, BF16),
+            pltpu.VMEM((SIDE,) + tile, BF16),
+            pltpu.VMEM((SIDE - 1,) + tile, BF16),
             pltpu.VMEM(tile, F32),
             pltpu.VMEM((16, 256), F32),
-            pltpu.SemaphoreType.DMA,
-            pltpu.SemaphoreType.DMA,
-            many, many, many, many, many, many,
+            pltpu.SemaphoreType.DMA((3,)),
+            pltpu.SemaphoreType.DMA((3,)),
+            hops, hops, hops, hops,
+            pltpu.SemaphoreType.DMA((3, SIDE)),
+            pltpu.SemaphoreType.DMA((3, SIDE)),
         ],
         compiler_params=pltpu.CompilerParams(
-            collective_id=1, has_side_effects=True, vmem_limit_bytes=32 << 20
+            collective_id=1, has_side_effects=True, vmem_limit_bytes=50 << 20
         ),
-    )(grads, first_low, second_low, first_top, second_top)
+    )(
+        x, weights_low, weights_top, adjacency_top, adjacency_top.T, labels[:, None],
+        ml, vl, mt, vt,
+    )
 
 
 def finish_kernel(steps, wl, wt, wl_out, wt_out):
@@ -538,12 +621,11 @@
     x = fetch(owners, slots, entries, features)
     members = lax.axis_size(("store", "rep"))
     scale = 1.0 / (labels.shape[0] * members)
-    logits, grads = local_step(x, weights_low, weights_top, adjacency_top, labels, scale)
-    grads = grads.reshape(STORES, 2, 16, grads.shape[1])
-    steps, new_first_low, new_second_low, new_first_top, new_second_top = reduce_and_update(
-        grads, first_low, second_low, first_top, second_top
-    )
-    new_low, new_top = finish(steps.reshape(-1, grads.shape[3]), weights_low, weights_top)
+    logits, steps, new_first_low, new_second_low, new_first_top, new_second_top = train(
+        x, weights_low, weights_top, adjacency_top, labels, scale,
+        first_low, second_low, first_top, second_top,
+    )
+    new_low, new_top = finish(steps.reshape(-1, steps.shape[-1]), weights_low, weights_top)
     return (logits, new_low, new_first_low, new_second_low, new_top, new_first_top, new_second_top)
 
 

time: 278 us -> 256 us (0.921)
  Pallas kernels: 256 us -> 234 us
    pallas_call x2 -> x1, Pallas kernels: 84.4 us -> 61.9 us  [train(): pl.pallas_call(functools.partial(train_kernel, scale), out_shape=(jax.Sha...]
    unnamed x28 -> x30, local copies, waits for them, and re-layouts: 15.4 us -> 16.2 us
where the time goes in v2:
time: 256 us
  Pallas kernels  234 us (91%)
  local copies, waits for them, and re-layouts  19 us (7%)
    pallas_call x1, Pallas kernels, fetch(): pl.pallas_call(fetch_kernel, out_shape=jax.ShapeDtypeStruct((near, 2 * wi...  168 us
    pallas_call x1, Pallas kernels, train(): pl.pallas_call(functools.partial(train_kernel, scale), out_shape=(jax.Sha...  61.9 us
    unnamed x30, local copies, waits for them, and re-layouts  16.2 us

profile of v2, /device:TPU:1, one launch (start us, length us, event | category | flops | bytes accessed | tf_op | source)
XLA Modules:
  0.0 255.9 jit_solution(6083733881026634793)
XLA Ops:
  0.6 0.7 pad_add_fusion.1
  1.4 0.6 broadcast_in_dim.10.own
  2.0 0.7 pad_add_fusion.2
  2.7 0.6 broadcast_in_dim.11.slots
  3.3 0.8 pad_add_fusion
  4.1 0.8 copy.31.lab
  4.8 0.8 copy.30.at
  5.6 0.8 copy.28.adj
  6.5 0.0 copy-start.10
  6.5 167.7 %shard_map.189.x = bf16[512,1536]{1,0:T(8,128)(2,1)} custom-call(s32[1,3584]{1,0:T(1,128)} %broadcast_in_dim.10.own, s32[1,3584]{1,0:T(1,128)} %broadcast_in_dim.11.slots, s32[512,16]{1,0:T(8,128)} %copy.28.adj, bf16[2048,768]{1,0:T(8,128)(2,1)} %feat.1), custom_call_target="tpu_custom_call" | custom-call | tf_op jit(solution)/shard_map/pallas_call | solution.py:215
  174.2 0.0 copy-done.10
  174.2 0.0 copy-start.5
  174.2 0.0 copy-start.6
  174.2 0.0 copy-start.7
  174.3 0.0 copy-start.8
  174.3 0.0 copy-start.9
  174.3 1.8 copy.29.wt
  176.0 0.0 copy-done.5
  176.1 0.0 copy-done.6
  176.1 0.0 copy-done.7
  176.1 0.0 copy-done.8
  176.1 0.0 copy-done.9
  176.1 0.0 copy-start.2
  176.1 1.4 copy-done.2
  177.5 0.0 copy-start.1
  177.5 61.9 %shard_map.190 = (f32[128,153]{1,0:T(8,128)S(1)}, bf16[4,4,4,2,16,1024]{5,4,3,2,1,0:T(8,128)(2,1)}, f32[12,1024]{1,0:T(8,128)S(1)}, f32[12,1024]{1,0:T(8,128)S(1...) custom-call(bf16[512,1536]{1,0:T(8,128)(2,1)S(1)} %copy-done.2, f32[1536,1024]{1,0:T(8,128)} %wl.3, ...), custom_call_target="tpu_custom_call" | custom-call | tf_op jit(solution)/shard_map/pallas_call | solution.py:532
  239.4 0.7 copy.33
  240.2 0.0 copy-done.1
  240.2 0.0 copy-start
  240.2 2.8 %copy-done = f32[1536,1024]{1,0:T(8,128)S(1)} copy-done((f32[1536,1024]{1,0:T(8,128)S(1)}, f32[1536,1024]{1,0:T(8,128)}, u32[]{:S(2)}) %copy-start) | copy-done | bytes 6291480
  242.9 0.0 copy-start.3
  243.0 2.2 copy-done.3
  245.1 4.3 %shard_map.191 = (f32[1536,1024]{1,0:T(8,128)}, f32[2048,153]{1,0:T(8,128)S(1)}) custom-call(bf16[2048,1024]{1,0:T(8,128)(2,1)S(1)} %bitcast.7, f32[1536,1024]{1,0:T(8,128)S(1)} %copy-done, f32[2048,153]{1,0:T(8,128)S(1)} %copy-done.1), custom_call_target="tpu_custom_call" | custom-call | tf_op jit(solution)/shard_map/pallas_call | solution.py:588
  249.4 0.0 copy-start.4
  249.4 1.3 copy-done.4
  250.8 2.7 %copy.34 = f32[2048,153]{0,1:T(8,128)} copy(f32[2048,153]{1,0:T(8,128)} %copy-done.4) | data formatting | bytes 2506752
  253.5 0.6 copy.39
  254.1 0.6 copy.40
  254.7 0.6 copy.41
  255.3 0.6 copy.42
  (1 shorter events, 0.0 us)
Async XLA Ops:
  6.5 167.8 %copy-start.10 = (f32[2048,153]{0,1:T(8,128)S(1)}, f32[2048,153]{0,1:T(8,128)}, u32[]{:S(2)}) copy-start(f32[2048,153]{0,1:T(8,128)} %param.23) | copy-start | bytes 3760132
  174.2 1.8 copy-start.5
  174.2 1.8 copy-start.6
  174.2 1.8 copy-start.7
  174.3 1.8 copy-start.8
  174.3 1.8 copy-start.9
  176.1 1.4 copy-start.2
  177.5 62.7 %copy-start.1 = (f32[2048,153]{1,0:T(8,128)S(1)}, f32[2048,153]{1,0:T(8,128)}, u32[]{:S(2)}) copy-start(f32[2048,153]{1,0:T(8,128)} %copy.29.wt) | copy-start | bytes 3760132
  240.2 2.8 %copy-start = (f32[1536,1024]{1,0:T(8,128)S(1)}, f32[1536,1024]{1,0:T(8,128)}, u32[]{:S(2)}) copy-start(f32[1536,1024]{1,0:T(8,128)} %wl.3) | copy-start | bytes 18874372
  242.9 2.2 copy-start.3
  249.4 1.3 copy-start.4

commit v3 on v2

v3 whole, which is shorter than its diff:
```python
import functools

import jax
import jax.numpy as jnp
from jax import lax
from jax.experimental import pallas as pl
from jax.experimental.pallas import tpu as pltpu
from jax.sharding import PartitionSpec as P

beta_one = 0.9
beta_two = 0.999
bias_one = 1.0 - 0.9**10
bias_two = 1.0 - 0.999**10
learn_rate = 0.01
adam_eps = 1e-08

MESH = pl.DeviceIdType.MESH
F32 = jnp.float32
BF16 = jnp.bfloat16
SIDE = 4
STORES = SIDE**3
CAP_NEAR = 16
CAP_FAR = 96
CAP = CAP_NEAR + CAP_FAR


def iota(shape, dim):
    return lax.broadcasted_iota(jnp.int32, shape, dim)


def dot(a, b):
    return jnp.dot(a, b, preferred_element_type=F32)


def dot_nt(a, b):
    return lax.dot_general(a, b, (((1,), (1,)), ((), ())), preferred_element_type=F32)


def place():
    store = lax.axis_index("store")
    return (store // 16, lax.rem(store // 4, 4), lax.rem(store, 4)), lax.axis_index("rep")


def at(chip):
    return (chip[0] * SIDE + chip[1]) * SIDE + chip[2]


def moved(chip, axis, step):
    return [lax.rem(c + step, SIDE) if n == axis else c for n, c in enumerate(chip)]


def partner(shift, chip, sign):
    steps = (shift // 16, lax.rem(shift // 4, 4), lax.rem(shift, 4))
    return at([lax.rem(c + sign * step + SIDE, SIDE) for c, step in zip(chip, steps)])


def routes():
    load = [[0] * 3 for _ in range(3)]
    found = {}
    by_hops = {1: [], 2: [], 3: []}
    for shift in range(1, STORES):
        steps = (shift // 16, shift // 4 % 4, shift % 4)
        by_hops[sum(step != 0 for step in steps)].append((shift, steps))
    for hops in (3, 2, 1):
        for shift, steps in by_hops[hops]:
            options = [
                [axis for axis in order if steps[axis]]
                for order in ((0, 1, 2), (1, 2, 0), (2, 0, 1), (0, 2, 1), (2, 1, 0), (1, 0, 2))
            ]
            cost = lambda order: sum(
                load[h][axis] * min(steps[axis], SIDE - steps[axis]) * (3 - h)
                for h, axis in enumerate(order)
            )
            order = min(options, key=cost)
            for h, axis in enumerate(order):
                load[h][axis] += min(steps[axis], SIDE - steps[axis])
            found[shift] = [(axis, steps[axis]) for axis in order]
    return found, *([shift for shift, _ in by_hops[hops]] for hops in (3, 2, 1))


ROUTES, THREE, TWO, ONE = routes()
LEAVE = THREE + TWO + ONE + [0]
ARRIVE = [0] + ONE + [shift for both in zip(TWO, THREE) for shift in both]
SEGMENTS = (1, 2, 4, 9)
GROUPS = 8


def fetch_kernel(
    own_near, slot_near, own_far, slot_far, adj, spots, feat, out,
    table, cols, chosen, req_out, req_in, asked, counts, selves, send, relay_one, relay_two, recv,
    total, marks,
    ask_send, ask_recv, send_one, send_two, send_three, recv_one, recv_two, recv_three,
):
    chip, rep = place()
    barrier = pltpu.get_barrier_semaphore()

    @pl.loop(1, STORES)
    def _(shift):
        pl.semaphore_signal(
            barrier, inc=1, device_id=(partner(shift, chip, 1), rep), device_id_type=MESH
        )

    table[...] = jnp.zeros_like(table)
    upper = (iota((256, 256), 0) < iota((256, 256), 1)).astype(BF16)
    base = jnp.zeros((STORES, 1), F32)
    high = jnp.zeros((STORES, 128), F32)
    low = jnp.zeros((STORES, 128), F32)
    near_rows = own_near.shape[1]
    near_blocks = near_rows // 256
    spot = spots[:, 0:1]
    for b in range(near_blocks + own_far.shape[1] // 256):
        far = b >= near_blocks
        if b == near_blocks:
            base = jnp.zeros((STORES, 1), F32)
        first = 256 * (b - near_blocks if far else b)
        owner = (own_far if far else own_near)[:, first : first + 256]
        wanted = (slot_far if far else slot_near)[:, first : first + 256]
        jx = (chip[0] - (owner >> 4)) & 3
        jy = (chip[1] - ((owner >> 2) & 3)) & 3
        jz = (chip[2] - (owner & 3)) & 3
        shift = jx * 16 + jy * 4 + jz
        owned = (iota((STORES, 256), 0) == shift).astype(F32)
        owned_bf = owned.astype(BF16)
        before = dot(owned_bf, upper) + base
        base = base + jnp.sum(owned, axis=1, keepdims=True)
        position = jnp.sum(owned * before, axis=0, keepdims=True)
        if far:
            position = position + CAP_NEAR
        arrival = jnp.sum(owned * spot, axis=0, keepdims=True)
        for half in range(2):
            part = slice(128 * half, 128 * half + 128)
            table[2 * b + half : 2 * b + half + 1, 0:128] = arrival[:, part]
            table[2 * b + half : 2 * b + half + 1, 128:256] = position[:, part]
        placed = (iota((128, 256), 0) == position.astype(jnp.int32)).astype(F32)
        high = high + dot_nt(owned_bf, (placed * (wanted >> 6).astype(F32)).astype(BF16))
        low = low + dot_nt(owned_bf, (placed * (wanted & 63).astype(F32)).astype(BF16))
    requests = (high * 64.0 + low).astype(jnp.int32)
    for shift in range(STORES):
        req_out[shift] = requests[shift : shift + 1, :]
    req_in[0] = requests[0:1, :]

    pl.semaphore_wait(barrier, STORES - 1)

    def ask(shift):
        return pltpu.make_async_remote_copy(
            src_ref=req_out.at[shift], dst_ref=req_in.at[shift],
            send_sem=ask_send.at[shift], recv_sem=ask_recv.at[shift],
            device_id=(partner(shift, chip, -1), rep), device_id_type=MESH,
        )

    @pl.loop(1, STORES)
    def _(shift):
        ask(shift).start()

    table_t = jnp.transpose(table[...]).astype(BF16)
    fan = adj.shape[0]
    cols[...] = jnp.zeros_like(cols)
    for k in range(fan + 1):
        entry = adj[k : k + 1, :] if k < fan else iota((1, near_rows), 1)
        row_mark = (iota((128, near_rows), 0) == (entry >> 7)).astype(F32).astype(BF16)
        found = dot(table_t, row_mark)
        column = found[0:128] * float(CAP if k < fan else CAP_NEAR) + found[128:256]
        picked = iota((128, near_rows), 0) == (entry & 127)
        cols[k : k + 1, :] = jnp.sum(jnp.where(picked, column, 0.0), axis=0, keepdims=True)
    for c in range(near_rows // 128):
        block = slice(128 * c, 128 * c + 128)
        chosen[block, :] = jnp.transpose(cols[:, block])

    @pl.loop(1, STORES)
    def _(shift):
        ask(shift).wait()

    lists = jnp.concatenate(
        [req_in[shift].astype(F32) for shift in LEAVE] + [jnp.zeros((64, 128), F32)], axis=0
    )
    asked[...] = jnp.transpose(lists)[0:CAP, :]

    hops = {}

    def go(shift, hop):
        route = ROUTES[shift]
        if hop == 0:
            src = send.at[LEAVE.index(shift)]
        elif hop == 1:
            src = relay_one.at[LEAVE.index(shift)]
        else:
            src = relay_two.at[LEAVE.index(shift)]
        if hop == len(route) - 1:
            dst = recv.at[ARRIVE.index(shift)]
        elif hop == 0:
            dst = relay_one.at[LEAVE.index(shift)]
        else:
            dst = relay_two.at[LEAVE.index(shift)]
        hops[shift, hop] = pltpu.make_async_remote_copy(
            src_ref=src, dst_ref=dst,
            send_sem=(send_one, send_two, send_three)[hop].at[shift],
            recv_sem=(recv_one, recv_two, recv_three)[hop].at[shift],
            device_id=(at(moved(chip, *route[hop])), rep), device_id_type=MESH,
        )
        hops[shift, hop].start()

    nodes = feat.shape[0]

    def pick(g):
        for m in range(4):
            lane = iota((CAP, 128), 1) == g * 4 + m
            row = jnp.sum(jnp.where(lane, asked[...], 0.0), axis=1, keepdims=True)
            row = row.astype(jnp.int32)
            for c in range(nodes // 512):
                marks[CAP * m : CAP * m + CAP, 512 * c : 512 * c + 512] = (
                    (iota((CAP, 512), 1) + 512 * c == row).astype(F32).astype(BF16)
                )
        for h in range(3):
            span = slice(256 * h, 256 * h + 256)
            rows = dot(marks[...], feat[:, span]).astype(BF16)
            for m in range(4):
                send[g * 4 + m, :, span] = rows[CAP * m : CAP * m + CAP]

    begin = 0
    for size in SEGMENTS:
        pl.loop(begin, begin + size)(pick)
        for shift in LEAVE[4 * begin : 4 * (begin + size)]:
            if shift and (shift in THREE or shift in TWO):
                go(shift, 0)
        begin += size
    recv[0] = send[STORES - 1]
    for shift in THREE:
        hops[shift, 0].wait_recv()
        go(shift, 1)
    for shift in ONE:
        go(shift, 0)

    width = counts.shape[2]

    @pl.loop(0, near_rows // 32)
    def _(r):
        rows = pl.ds(pl.multiple_of(r * 32, 32), 32)
        picked = chosen[rows, :]
        for c in range(GROUPS):
            lane = (iota((32, width), 1) + width * c).astype(F32)
            tally = jnp.zeros((32, width), F32)
            for k in range(fan):
                tally = tally + jnp.where(lane == picked[:, k : k + 1], 1.0, 0.0)
            counts[c, rows, :] = tally.astype(BF16)
            lane = (iota((32, 128), 1) + 128 * c).astype(F32)
            selves[c, rows, :] = jnp.where(lane == picked[:, fan : fan + 1], 1.0, 0.0).astype(BF16)

    for shift in TWO:
        hops[shift, 0].wait_recv()
        go(shift, 1)
    for shift in THREE:
        hops[shift, 1].wait_recv()
        go(shift, 2)

    features = recv.shape[2]
    many = STORES // GROUPS
    for c in range(GROUPS):
        for shift in ARRIVE[many * c : many * (c + 1)]:
            if shift:
                hops[shift, len(ROUTES[shift]) - 1].wait_recv()
        for h in range(3):
            span = slice(256 * h, 256 * h + 256)
            block = recv[many * c : many * (c + 1), :, span].reshape(width, 256)
            nears = recv[many * c : many * (c + 1), 0:CAP_NEAR, span].reshape(128, 256)
            sums = dot(counts[c], block)
            same = dot(selves[c], nears).astype(BF16)
            if c:
                sums = sums + total[:, span]
                same = same + out[:, span]
            out[:, span] = same
            if c < GROUPS - 1:
                total[:, span] = sums
            else:
                out[:, features + 256 * h : features + 256 * h + 256] = (
                    sums / float(fan)
                ).astype(BF16)
    for made in hops.values():
        made.wait_send()


def fetch(owners_near, slots_near, owners_far, slots_far, adjacency, features):
    near = adjacency.shape[1]
    width = features.shape[1]
    vmem = pl.BlockSpec(memory_space=pltpu.VMEM)
    spots = jnp.array([[ARRIVE.index(shift)] * 128 for shift in range(STORES)], F32)
    rows = (CAP, width)
    many = pltpu.SemaphoreType.DMA((STORES,))
    return pl.pallas_call(
        fetch_kernel,
        out_shape=jax.ShapeDtypeStruct((near, 2 * width), BF16),
        in_specs=[vmem] * 7,
        out_specs=vmem,
        scratch_shapes=[
            pltpu.VMEM((128, 256), F32),
            pltpu.VMEM((128, near), F32),
            pltpu.VMEM((near, 128), F32),
            pltpu.VMEM((STORES, 1, 128), jnp.int32),
            pltpu.VMEM((STORES, 1, 128), jnp.int32),
            pltpu.VMEM((CAP, 128), F32),
            pltpu.VMEM((GROUPS, near, STORES // GROUPS * CAP), BF16),
            pltpu.VMEM((GROUPS, near, 128), BF16),
            pltpu.VMEM((STORES,) + rows, BF16),
            pltpu.VMEM((len(THREE) + len(TWO),) + rows, BF16),
            pltpu.VMEM((len(THREE),) + rows, BF16),
            pltpu.VMEM((STORES,) + rows, BF16),
            pltpu.VMEM((near, width), F32),
            pltpu.VMEM((4 * CAP, features.shape[0]), BF16),
            many, many, many, many, many, many, many, many,
        ],
        compiler_params=pltpu.CompilerParams(
            collective_id=0, has_side_effects=True, vmem_limit_bytes=60 << 20
        ),
    )(owners_near, slots_near, owners_far, slots_far, adjacency, spots, features)


def spread_low():
    row, column = iota((384, 512), 0), iota((384, 512), 1)
    inner = column & 15
    return ((inner < 12) & (row == 12 * (column >> 4) + inner)).astype(F32).astype(BF16)


def spread_low_t():
    column, row = iota((512, 384), 1), iota((512, 384), 0)
    inner = row & 15
    return ((inner < 12) & (column == 12 * (row >> 4) + inner)).astype(F32).astype(BF16)


def spread_top(b):
    row, column = iota((256, 256), 0), iota((256, 256), 1)
    inner = column & 15
    return (
        ((inner >= 12) & (row == (column & -16) + 4 * (inner - 12) + b)).astype(F32).astype(BF16)
    )


def spread_top_t(b):
    column, row = iota((256, 256), 1), iota((256, 256), 0)
    inner = row & 15
    return (
        ((inner >= 12) & (column == (row & -16) + 4 * (inner - 12) + b)).astype(F32).astype(BF16)
    )


def gelu_parts(v):
    root = 0.7978845608028654
    square = v * v
    t = jnp.tanh(root * (v + 0.044715 * (v * square)))
    gate = 0.5 * (1.0 + t)
    slope = gate + 0.5 * v * (1.0 - t * t) * (root * (1.0 + 3.0 * 0.044715 * square))
    return v * gate, slope


def step_part(scale, x, wl, wt_t, at_t, lab, logits_out, grads, wtb, hidden, slope, dpre, left):
    classes = wt_t.shape[0]
    width = wl.shape[1]
    fan, seeds = at_t.shape
    near = x.shape[0]
    wtb[...] = jnp.zeros_like(wtb)
    wtb[0:classes, :] = wt_t[...].astype(BF16)
    for n in range(width // 256):
        span = slice(256 * n, 256 * n + 256)
        value, rise = gelu_parts(dot(x[...], wl[:, span].astype(BF16)))
        hidden[:, span] = value.astype(BF16)
        slope[:, span] = rise
    picks_t = jnp.zeros((near, seeds), F32)
    for k in range(fan):
        picks_t = picks_t + (iota((near, seeds), 0) == at_t[k : k + 1, :]).astype(F32)
    picks = jnp.transpose(picks_t).astype(BF16)
    picks_t = picks_t.astype(BF16)
    mean = (dot(picks, hidden[...]) / float(fan)).astype(BF16)
    own = hidden[0:seeds, :]
    logits = dot_nt(wtb[:, 0:width], own) + dot_nt(wtb[:, width : 2 * width], mean)
    logits_out[...] = logits[0:classes]
    line = iota(logits.shape, 0)
    powers = jnp.where(line < classes, jnp.exp(logits), 0.0)
    chances = powers / jnp.sum(powers, axis=0, keepdims=True)
    targets = (line == lab[...]).astype(F32)
    dlogits = jnp.transpose((chances - targets) * scale).astype(BF16)
    first = dot(dlogits, wtb[:, 0:width])
    second = dot(dlogits, wtb[:, width : 2 * width]) / float(fan)
    second_high = second.astype(BF16)
    second_low = (second - second_high.astype(F32)).astype(BF16)
    for n in range(width // 256):
        span = slice(256 * n, 256 * n + 256)
        back = dot(picks_t, second_high[:, span]) + dot(picks_t, second_low[:, span])
        dpre[seeds:near, span] = (back[seeds:near] * slope[seeds:near, span]).astype(BF16)
        dpre[0:seeds, span] = ((back[0:seeds] + first[:, span]) * slope[0:seeds, span]).astype(BF16)
    low_t = spread_low_t()
    for m in range(x.shape[1] // 384):
        left[512 * m : 512 * m + 512, :] = dot_nt(low_t, x[:, 384 * m : 384 * m + 384]).astype(BF16)
    for b in range(width // 256):
        span = slice(256 * b, 256 * b + 256)
        top_t = spread_top_t(b)
        for m in range(2 * width // 256):
            source = own if m < width // 256 else mean
            at_col = 256 * (m % (width // 256))
            top_left = dot_nt(top_t, source[:, at_col : at_col + 256]).astype(BF16)
            rows = slice(256 * m, 256 * m + 256)
            block = dot(left[rows, :], dpre[:, span]) + dot(top_left, dlogits)
            grads[m // 2, 2 * (m % 2) : 2 * (m % 2) + 2, :, :, :, span] = block.astype(BF16).reshape(
                2, SIDE, 2, 16, 256
            )


def adam_parts(moment, square, gradient):
    moment_new = beta_one * moment + (1.0 - beta_one) * gradient
    square_new = beta_two * square + (1.0 - beta_two) * gradient * gradient
    update = moment_new / bias_one / (jnp.sqrt(square_new / bias_two) + adam_eps)
    return learn_rate * update, moment_new, square_new


SPANS = (slice(0, 384), slice(384, 768), slice(768, 1024))


def top_rows(share, top):
    for a in range(4):
        for b in range(4):
            top[4 * a + b : 4 * a + b + 1, :] = share[12 + a : 13 + a, 256 * b : 256 * b + 256]


def block_of(axes, fixed, tail):
    return tuple(fixed.get(axis, slice(None)) for axis in axes) + tail


def reduce_part(
    chip, rep, grads, ml, vl, mt, vt, everyone, gradient_out,
    pair, halves, got_one, sum_one, got_two, sum_two, got_three, share, top,
    pair_send, pair_recv, down_send, down_recv, up_send, up_recv, twin_send, twin_recv,
):
    other = 1 - rep
    classes = mt.shape[1]
    every = slice(None)

    def copy(src, dst, send_sem, recv_sem, to, core):
        return pltpu.make_async_remote_copy(
            src_ref=src, dst_ref=dst, send_sem=send_sem, recv_sem=recv_sem,
            device_id=(at(to), core), device_id_type=MESH,
        )

    swaps = []
    for c, span in enumerate(SPANS):
        swaps.append(copy(
            grads.at[:, :, :, other, :, span], pair.at[:, :, :, :, span],
            pair_send.at[c], pair_recv.at[c], chip, other,
        ))
        swaps[c].start()
    sent = list(swaps)
    got = (got_one, got_two, got_three)
    waiting = []
    for c, span in enumerate(SPANS):
        swaps[c].wait_recv()

        @pl.loop(0, SIDE)
        def _(x):
            for y in range(SIDE):
                for z in range(SIDE):
                    halves[x, y, z, :, span] = (
                        grads[x, y, z, rep, :, span].astype(F32) + pair[x, y, z, :, span].astype(F32)
                    ).astype(BF16)

        axes, first = (0, 1, 2), c
        copies = []
        for k in range(1, SIDE):
            to = moved(chip, first, k)
            copies.append(copy(
                halves.at[block_of(axes, {first: to[first]}, (every, span))],
                got_one.at[k - 1, :, :, :, span],
                down_send.at[0, c, k - 1], down_recv.at[0, c, k - 1], to, rep,
            ))
            copies[-1].start()
        sent += copies
        waiting.append(copies)
    following = []
    for c, span in enumerate(SPANS):
        first, second = c, (c + 1) % 3
        left = tuple(n for n in range(3) if n != first)
        for made in waiting[c]:
            made.wait_recv()
        for a in range(SIDE):
            for b in range(SIDE):
                spot = {left[0]: a, left[1]: b, first: chip[first]}
                total = halves[block_of((0, 1, 2), spot, (every, span))].astype(F32)
                for k in range(1, SIDE):
                    total = total + got_one[k - 1, a, b, :, span].astype(F32)
                sum_one[a, b, :, span] = total.astype(BF16)
        copies = []
        for k in range(1, SIDE):
            to = moved(chip, second, k)
            copies.append(copy(
                sum_one.at[block_of(left, {second: to[second]}, (every, span))],
                got_two.at[k - 1, :, :, span],
                down_send.at[1, c, k - 1], down_recv.at[1, c, k - 1], to, rep,
            ))
            copies[-1].start()
        sent += copies
        following.append(copies)
    waiting, following = following, []
    for c, span in enumerate(SPANS):
        first, second, third = c, (c + 1) % 3, (c + 2) % 3
        left = tuple(n for n in range(3) if n != first)
        for made in waiting[c]:
            made.wait_recv()
        for a in range(SIDE):
            spot = {third: a, second: chip[second]}
            total = sum_one[block_of(left, spot, (every, span))].astype(F32)
            for k in range(1, SIDE):
                total = total + got_two[k - 1, a, :, span].astype(F32)
            sum_two[a, :, span] = total.astype(BF16)
        copies = []
        for k in range(1, SIDE):
            to = moved(chip, third, k)
            copies.append(copy(
                sum_two.at[to[third], :, span], got_three.at[k - 1, :, span],
                down_send.at[2, c, k - 1], down_recv.at[2, c, k - 1], to, rep,
            ))
            copies[-1].start()
        sent += copies
        following.append(copies)
    for c, span in enumerate(SPANS):
        for made in following[c]:
            made.wait_recv()
        total = sum_two[chip[(c + 2) % 3], :, span].astype(F32)
        for k in range(1, SIDE):
            total = total + got_three[k - 1, :, span].astype(F32)
        share[:, span] = total

    gradient_out[...] = share[...]
    top_rows(share, top)
    share[0:12, :] = adam_parts(ml[...], vl[...], share[0:12, :])[0]
    step = adam_parts(mt[...], vt[...], top[:, 0:classes])[0]
    top[:, 0:classes] = step
    for a in range(4):
        for b in range(4):
            share[12 + a : 13 + a, 256 * b : 256 * b + 256] = top[4 * a + b : 4 * a + b + 1, :]
    everyone[chip[0], chip[1], chip[2], rep] = share[...].astype(BF16)

    waiting = [[] for span in SPANS]
    twins = []
    for level in range(4):
        for c, span in enumerate(SPANS):
            order = ((c + 2) % 3, (c + 1) % 3, c)
            for made in waiting[c]:
                made.wait_recv()
            if level < 3:
                spot = {n: chip[n] for n in order[level:]}
                block = everyone.at[block_of((0, 1, 2), spot, (rep, every, span))]
                waiting[c] = []
                for k in range(1, SIDE):
                    waiting[c].append(copy(
                        block, block, up_send.at[level, c, k - 1], up_recv.at[level, c, k - 1],
                        moved(chip, order[level], k), rep,
                    ))
                    waiting[c][-1].start()
                sent += waiting[c]
            if level >= 2:
                for k in range(1 if level == 3 else 0, SIDE if level == 3 else 1):
                    spot = {c: lax.rem(chip[c] + SIDE - k, SIDE)}
                    block = everyone.at[block_of((0, 1, 2), spot, (rep, every, span))]
                    twins.append(copy(
                        block, block, twin_send.at[c, k], twin_recv.at[c, k], chip, other
                    ))
                    twins[-1].start()
    for made in twins:
        made.wait()
    for made in sent:
        made.wait_send()


def train_kernel(
    scale, x, wl, wt_t, at_t, lab, ml, vl, mt, vt, logits_out, everyone, gradient_out,
    wtb, hidden, slope, dpre, left, grads, *scratch,
):
    chip, rep = place()
    barrier = pltpu.get_barrier_semaphore()
    for axis in range(3):
        for k in range(1, SIDE):
            to = at(moved(chip, axis, k))
            pl.semaphore_signal(barrier, inc=1, device_id=(to, rep), device_id_type=MESH)
    pl.semaphore_signal(
        barrier, inc=1, device_id=(lax.axis_index("store"), 1 - rep), device_id_type=MESH
    )
    step_part(scale, x, wl, wt_t, at_t, lab, logits_out, grads, wtb, hidden, slope, dpre, left)
    pl.semaphore_wait(barrier, 10)
    reduce_part(chip, rep, grads, ml, vl, mt, vt, everyone, gradient_out, *scratch)


def train(x, weights_low, top_t, adjacency_t, labels, scale, ml, vl, mt, vt):
    near = x.shape[0]
    seeds = adjacency_t.shape[1]
    width = weights_low.shape[1]
    cube = (SIDE, SIDE, SIDE)
    tile = (16, width)
    vmem = pl.BlockSpec(memory_space=pltpu.VMEM)
    hops = pltpu.SemaphoreType.DMA((3, 3, 3))
    return pl.pallas_call(
        functools.partial(train_kernel, scale),
        out_shape=(
            jax.ShapeDtypeStruct((top_t.shape[0], seeds), F32),
            jax.ShapeDtypeStruct(cube + (2,) + tile, BF16),
            jax.ShapeDtypeStruct(tile, F32),
        ),
        in_specs=[vmem] * 9,
        out_specs=(vmem,) * 3,
        scratch_shapes=[
            pltpu.VMEM((256, 2 * width), BF16),
            pltpu.VMEM((near, width), BF16),
            pltpu.VMEM((near, width), F32),
            pltpu.VMEM((near, width), BF16),
            pltpu.VMEM((2 * width, near), BF16),
            pltpu.VMEM(cube + (2,) + tile, BF16),
            pltpu.VMEM(cube + tile, BF16),
            pltpu.VMEM(cube + tile, BF16),
            pltpu.VMEM((SIDE - 1, SIDE, SIDE) + tile, BF16),
            pltpu.VMEM((SIDE, SIDE) + tile, BF16),
            pltpu.VMEM((SIDE - 1, SIDE) + tile, BF16),
            pltpu.VMEM((SIDE,) + tile, BF16),
            pltpu.VMEM((SIDE - 1,) + tile, BF16),
            pltpu.VMEM(tile, F32),
            pltpu.VMEM((16, 256), F32),
            pltpu.SemaphoreType.DMA((3,)),
            pltpu.SemaphoreType.DMA((3,)),
            hops, hops, hops, hops,
            pltpu.SemaphoreType.DMA((3, SIDE)),
            pltpu.SemaphoreType.DMA((3, SIDE)),
        ],
        compiler_params=pltpu.CompilerParams(
            collective_id=1, has_side_effects=True, vmem_limit_bytes=40 << 20
        ),
    )(x, weights_low, top_t, adjacency_t, labels, ml, vl, mt, vt)


def finish_kernel(
    steps, gradient, logits, wl, wt_t, ml, vl, mt, vt,
    logits_out, wl_out, wt_t_out, ml_out, vl_out, mt_out, vt_out, top,
):
    classes = wt_t.shape[0]
    wl_out[...] = wl[...] - dot(spread_low(), steps[...])
    for m in range(2):
        rows = slice(256 * m, 256 * m + 256)
        step = jnp.zeros((256, 256), F32)
        for b in range(4):
            step = step + dot(spread_top(b), steps[rows, 256 * b : 256 * b + 256])
        wt_t_out[:, rows] = wt_t[:, rows] - jnp.transpose(step)[0:classes]

    @pl.when(pl.program_id(0) == 0)
    def _():
        logits_out[...] = logits[...]
        _, ml_out[...], vl_out[...] = adam_parts(ml[...], vl[...], gradient[0:12, :])
        top_rows(gradient, top)
        _, mt_out[...], vt_out[...] = adam_parts(mt[...], vt[...], top[:, 0:classes])


def finish(steps, gradient, logits, weights_low, top_t, ml, vl, mt, vt):
    rows, width = weights_low.shape
    classes, tops = top_t.shape
    low = pl.BlockSpec((384, width), lambda i: (i, 0))
    top = pl.BlockSpec((classes, 512), lambda i: (0, i))
    same = [pl.BlockSpec(each.shape, lambda i: (0, 0)) for each in (ml, vl, mt, vt)]
    share = pl.BlockSpec(gradient.shape, lambda i: (0, 0))
    scores = pl.BlockSpec(logits.shape, lambda i: (0, 0))
    return pl.pallas_call(
        finish_kernel,
        grid=(4,),
        out_shape=tuple(
            jax.ShapeDtypeStruct(each.shape, F32)
            for each in (logits, weights_low, top_t, ml, vl, mt, vt)
        ),
        in_specs=[pl.BlockSpec((512, width), lambda i: (i, 0)), share, scores, low, top] + same,
        out_specs=[scores, low, top] + same,
        scratch_shapes=[pltpu.VMEM((16, 256), F32)],
        compiler_params=pltpu.CompilerParams(vmem_limit_bytes=32 << 20),
    )(steps, gradient, logits, weights_low, top_t, ml, vl, mt, vt)


def per_device(
    features,
    owners_near,
    slots_near,
    owners_far,
    slots_far,
    adjacency_low,
    adjacency_top,
    labels,
    weights_low,
    weights_top,
    first_low,
    second_low,
    first_top,
    second_top,
):
    x = fetch(
        owners_near.T, slots_near.T, owners_far.T, slots_far.T, adjacency_low.T, features
    )
    members = lax.axis_size(("store", "rep"))
    scale = 1.0 / (labels.shape[0] * members)
    top_t = weights_top.T
    moments = (first_low, second_low, first_top, second_top)
    logits, steps, gradient = train(
        x, weights_low, top_t, adjacency_top.T, labels[None, :], scale, *moments
    )
    logits, new_low, new_top, new_first_low, new_second_low, new_first_top, new_second_top = finish(
        steps.reshape(-1, steps.shape[-1]), gradient, logits, weights_low, top_t, *moments
    )
    return (
        logits.T, new_low, new_first_low, new_second_low, new_top.T, new_first_top, new_second_top
    )


def solution(mesh):
    both = P(("store", "rep"), None)
    return jax.shard_map(
        per_device,
        mesh=mesh,
        in_specs=(
            P("store", None), both, both, both, both, both, both, P(("store", "rep")),
            P(), P(), both, both, both, both,
        ),
        out_specs=(both, P(), both, both, P(), both, both),
        check_vma=False,
    )
```

time: 256 us -> 224 us (0.88)
  Pallas kernels: 234 us -> 218 us
  local copies, waits for them, and re-layouts: 19 us -> 4.23 us
    unnamed x30 -> x22, local copies, waits for them, and re-layouts: 16.2 us -> 4.23 us
    pallas_call x1, Pallas kernels: 168 us -> 156 us  [fetch(): pl.pallas_call(fetch_kernel, out_shape=jax.ShapeDtypeStruct((near, 2 * wi...]
    pallas_call x1, Pallas kernels: 61.9 us -> 56.9 us  [train(): pl.pallas_call(functools.partial(train_kernel, scale), out_shape=(jax.Sha...]
where the time goes in v3:
time: 224 us
  Pallas kernels  218 us (97%)
  local copies, waits for them, and re-layouts  4.23 us (2%)
    pallas_call x1, Pallas kernels, fetch(): pl.pallas_call(fetch_kernel, out_shape=jax.ShapeDtypeStruct((near, 2 * wi...  156 us
    pallas_call x1, Pallas kernels, train(): pl.pallas_call(functools.partial(train_kernel, scale), out_shape=(jax.Sha...  56.9 us
    pallas_call x1, Pallas kernels, finish(): pl.pallas_call(finish_kernel, grid=(4,), out_shape=tuple((jax.ShapeDtypeS...  5.71 us

profile of v3, /device:TPU:1, one launch (start us, length us, event | category | flops | bytes accessed | tf_op | source)
XLA Modules:
  0.0 223.7 jit_solution(13120987293044690468)
XLA Ops:
  0.6 0.0 copy-start.6
  0.6 0.0 copy-start.5
  0.7 0.0 copy-start.4
  0.7 0.0 copy-start.3
  0.7 0.0 copy-start.2
  0.7 0.0 copy-start.8
  0.7 0.0 copy-start.7
  0.7 0.0 slice-start
  0.7 155.8 %shard_map.198.x = bf16[512,1536]{1,0:T(8,128)(2,1)} custom-call(s32[1,512]{1,0:T(1,128)} %bitcast.21, s32[1,512]{1,0:T(1,128)} %bitcast.22, s32[1,3072]{1,0:T(1,128)} %bitcast.19, s32[1,3072]{1,0:T(1,128)} %bitcast.20, s32[15,512]{1,0:T(8,128)} %bitcast.18, f32[64,128]{1,0:T(8,128)} %constant.2.clone.spots, bf16[2048,768]{1,0:T(8,128)(2,1)} %feat.1), custom_call_target="tpu_custom_call" | custom-call | tf_op jit(solution)/shard_map/pallas_call | solution.py:288
  156.6 0.0 copy-done.6
  156.6 0.0 copy-done.5
  156.6 0.0 copy-done.4
  156.6 0.0 copy-done.3
  156.6 0.0 copy-done.2
  156.6 0.0 copy-done.8
  156.6 0.0 copy-done.7
  156.6 0.0 copy-start
  156.7 2.8 %copy-done = f32[1536,1024]{1,0:T(8,128)S(1)} copy-done((f32[1536,1024]{1,0:T(8,128)S(1)}, f32[1536,1024]{1,0:T(8,128)}, u32[]{:S(2)}) %copy-start) | copy-done | bytes 6291480
  159.4 0.0 copy-start.1
  159.4 1.4 copy-done.1
  160.8 0.0 slice-start.1
  160.8 56.9 %shard_map.199 = (f32[153,128]{1,0:T(8,128)S(1)}, bf16[4,4,4,2,16,1024]{5,4,3,2,1,0:T(8,128)(2,1)S(1)}, f32[16,1024]{1,0:T(8,128)S(1)}) custom-call(bf16[512,1536]{1,0:T(8,128)(2,1)S(1)} %copy-done.1, f32[1536,1024]{1,0:T(8,128)S(1)} %copy-done, f32[153,2048]{1,0:T(8,128)S(1)} %bitcast.13, s32[10,128]{1,0:T(8,128)S(1)} %bitcast.16, s32[1,128]{1,0:T(1,128)S(1)} %bitcast.17, ...), custom_call_target="tpu_custom_call" | custom-call | tf_op jit(solution)/shard_map/pallas_call | solution.py:595
  217.8 0.0 slice-done
  217.8 0.0 slice-done.1
  217.8 5.7 %shard_map.200 = (f32[153,128]{1,0:T(8,128)}, f32[1536,1024]{1,0:T(8,128)}, f32[153,2048]{1,0:T(8,128)}, f32[12,1024]{1,0:T(8,128)}, f32[12,1024]{1,0:T(8,128)}, /*index=5*/f32[16,153]{1,0:T(8,128)}, f32[16,153]{1,0:T(8,128)}) custom-call(bf16[2048,1024]{1,0:T(8,128)(2,1)S(1)} %bitcast.15, f32[16,1024]{1,0:T(8,128)S(1)} %get-tuple-element.18.gradient, ...), custom_call_target="tpu_custom_call" | custom-call | tf_op jit(solution)/shard_map/pallas_call | solution.py:661
  (1 shorter events, 0.0 us)
Async XLA Ops:
  0.6 155.9 %copy-start.6 = (f32[16,153]{1,0:T(8,128)S(1)}, f32[16,153]{1,0:T(8,128)}, u32[]{:S(2)}) copy-start(f32[16,153]{1,0:T(8,128)} %vt.3) | copy-start | bytes 29380
  0.6 155.9 %copy-start.5 = (f32[16,153]{1,0:T(8,128)S(1)}, f32[16,153]{1,0:T(8,128)}, u32[]{:S(2)}) copy-start(f32[16,153]{1,0:T(8,128)} %mt.3) | copy-start | bytes 29380
  0.7 155.9 %copy-start.4 = (f32[12,1024]{1,0:T(8,128)S(1)}, f32[12,1024]{1,0:T(8,128)}, u32[]{:S(2)}) copy-start(f32[12,1024]{1,0:T(8,128)} %vl.3) | copy-start | bytes 147460
  0.7 155.9 %copy-start.3 = (f32[12,1024]{1,0:T(8,128)S(1)}, f32[12,1024]{1,0:T(8,128)}, u32[]{:S(2)}) copy-start(f32[12,1024]{1,0:T(8,128)} %ml.3) | copy-start | bytes 147460
  0.7 155.9 %copy-start.2 = (f32[2048,153]{0,1:T(8,128)S(1)}, f32[2048,153]{0,1:T(8,128)}, u32[]{:S(2)}) copy-start(f32[2048,153]{0,1:T(8,128)} %param.24) | copy-start | bytes 3760132
  0.7 155.9 %copy-start.8 = (s32[128]{0:T(128)S(1)}, s32[128]{0:T(128)}, u32[]{:S(2)}) copy-start(s32[128]{0:T(128)} %param.22) | copy-start | bytes 1540
  0.7 155.9 %copy-start.7 = (s32[128,10]{0,1:T(8,128)S(1)}, s32[128,10]{0,1:T(8,128)}, u32[]{:S(2)}) copy-start(s32[128,10]{0,1:T(8,128)} %param.21) | copy-start | bytes 15364
  0.7 217.1 %slice-start = ((s8[6291456]{0:T(1024)(128)(4,1)}), s8[2097152]{0:T(1024)(128)(4,1)S(1)}, s32[]{:S(2)}) async-start(s8[6291456]{0:T(1024)(128)(4,1)} %bitcast.11), calls=%async_computation | async-start | bytes 4194304
  156.6 2.8 %copy-start = (f32[1536,1024]{1,0:T(8,128)S(1)}, f32[1536,1024]{1,0:T(8,128)}, u32[]{:S(2)}) copy-start(f32[1536,1024]{1,0:T(8,128)} %wl.3) | copy-start | bytes 18874372
  159.4 1.4 copy-start.1
  160.8 56.9 %slice-start.1 = ((s8[6291456]{0:T(1024)(128)(4,1)}), s8[4194304]{0:T(1024)(128)(4,1)S(1)}, s32[]{:S(2)}) async-start(s8[6291456]{0:T(1024)(128)(4,1)} %bitcast.11), calls=%async_computation.1 | async-start | bytes 8388608

commit v4 on v3

--- a/solution.py
+++ b/solution.py
@@ -81,8 +81,17 @@
 ROUTES, THREE, TWO, ONE = routes()
 LEAVE = THREE + TWO + ONE + [0]
 ARRIVE = [0] + ONE + [shift for both in zip(TWO, THREE) for shift in both]
-SEGMENTS = (1, 2, 4, 9)
+SEGMENTS = (1, 2, 4, 4, 5)
 GROUPS = 8
+
+
+def load_all(stored, here, sem):
+    loads = [
+        pltpu.make_async_copy(src, dst, sem.at[n]) for n, (src, dst) in enumerate(zip(stored, here))
+    ]
+    for made in loads:
+        made.start()
+    return loads
 
 
 def fetch_kernel(
@@ -223,10 +232,10 @@
             if shift and (shift in THREE or shift in TWO):
                 go(shift, 0)
         begin += size
+        for shift in {11: THREE[:13], 16: THREE[13:]}.get(begin, []):
+            hops[shift, 0].wait_recv()
+            go(shift, 1)
     recv[0] = send[STORES - 1]
-    for shift in THREE:
-        hops[shift, 0].wait_recv()
-        go(shift, 1)
     for shift in ONE:
         go(shift, 0)
 
@@ -314,7 +323,7 @@
 
 
 def spread_low():
-    row, column = iota((384, 512), 0), iota((384, 512), 1)
+    row, column = iota((192, 256), 0), iota((192, 256), 1)
     inner = column & 15
     return ((inner < 12) & (row == 12 * (column >> 4) + inner)).astype(F32).astype(BF16)
 
@@ -350,16 +359,20 @@
     return v * gate, slope
 
 
-def step_part(scale, x, wl, wt_t, at_t, lab, logits_out, grads, wtb, hidden, slope, dpre, left):
+def step_part(
+    scale, x, strips, fetched, wt_t, at_t, lab, logits_out,
+    grads, wtb, hidden, slope, dpre, left, tops,
+):
     classes = wt_t.shape[0]
-    width = wl.shape[1]
+    width = hidden.shape[1]
     fan, seeds = at_t.shape
     near = x.shape[0]
     wtb[...] = jnp.zeros_like(wtb)
     wtb[0:classes, :] = wt_t[...].astype(BF16)
     for n in range(width // 256):
         span = slice(256 * n, 256 * n + 256)
-        value, rise = gelu_parts(dot(x[...], wl[:, span].astype(BF16)))
+        fetched[n].wait()
+        value, rise = gelu_parts(dot(x[...], strips[n].astype(BF16)))
         hidden[:, span] = value.astype(BF16)
         slope[:, span] = rise
     picks_t = jnp.zeros((near, seeds), F32)
@@ -389,17 +402,31 @@
     for m in range(x.shape[1] // 384):
         left[512 * m : 512 * m + 512, :] = dot_nt(low_t, x[:, 384 * m : 384 * m + 384]).astype(BF16)
     for b in range(width // 256):
-        span = slice(256 * b, 256 * b + 256)
         top_t = spread_top_t(b)
         for m in range(2 * width // 256):
             source = own if m < width // 256 else mean
             at_col = 256 * (m % (width // 256))
-            top_left = dot_nt(top_t, source[:, at_col : at_col + 256]).astype(BF16)
+            tops[b, 256 * m : 256 * m + 256, :] = dot_nt(
+                top_t, source[:, at_col : at_col + 256]
+            ).astype(BF16)
+
+    def gradient_span(span):
+        for m in range(2 * width // 256):
             rows = slice(256 * m, 256 * m + 256)
-            block = dot(left[rows, :], dpre[:, span]) + dot(top_left, dlogits)
+            block = dot(left[rows, :], dpre[:, span])
+            pieces = []
+            lane = span.start
+            while lane < span.stop:
+                b = lane // 256
+                stop = min(span.stop, 256 * b + 256)
+                pieces.append(dot(tops[b, rows, :], dlogits[:, lane - 256 * b : stop - 256 * b]))
+                lane = stop
+            block = block + (pieces[0] if len(pieces) == 1 else jnp.concatenate(pieces, axis=1))
             grads[m // 2, 2 * (m % 2) : 2 * (m % 2) + 2, :, :, :, span] = block.astype(BF16).reshape(
-                2, SIDE, 2, 16, 256
+                2, SIDE, 2, 16, span.stop - span.start
             )
+
+    return gradient_span
 
 
 def adam_parts(moment, square, gradient):
@@ -423,7 +450,7 @@
 
 
 def reduce_part(
-    chip, rep, grads, ml, vl, mt, vt, everyone, gradient_out,
+    gradient_span, chip, rep, grads, ml, vl, mt, vt, everyone, gradient_out,
     pair, halves, got_one, sum_one, got_two, sum_two, got_three, share, top,
     pair_send, pair_recv, down_send, down_recv, up_send, up_recv, twin_send, twin_recv,
 ):
@@ -438,16 +465,21 @@
         )
 
     swaps = []
-    for c, span in enumerate(SPANS):
+
+    def start_swap(c):
+        gradient_span(SPANS[c])
         swaps.append(copy(
-            grads.at[:, :, :, other, :, span], pair.at[:, :, :, :, span],
+            grads.at[:, :, :, other, :, SPANS[c]], pair.at[:, :, :, :, SPANS[c]],
             pair_send.at[c], pair_recv.at[c], chip, other,
         ))
         swaps[c].start()
-    sent = list(swaps)
-    got = (got_one, got_two, got_three)
+
+    sent = []
     waiting = []
+    start_swap(0)
     for c, span in enumerate(SPANS):
+        if c < 2:
+            start_swap(c + 1)
         swaps[c].wait_recv()
 
         @pl.loop(0, SIDE)
@@ -562,14 +594,27 @@
                     twins[-1].start()
     for made in twins:
         made.wait()
-    for made in sent:
+    for made in sent + swaps:
         made.wait_send()
 
 
 def train_kernel(
-    scale, x, wl, wt_t, at_t, lab, ml, vl, mt, vt, logits_out, everyone, gradient_out,
-    wtb, hidden, slope, dpre, left, grads, *scratch,
+    scale, x, wl, *refs,
 ):
+    stored, (logits_out, everyone, gradient_out), refs = refs[:7], refs[7:10], refs[10:]
+    here, load_sem, strips, strip_sem, refs = refs[:7], refs[7], refs[8], refs[9], refs[10:]
+    wt_t, at_t, lab, ml, vl, mt, vt = here
+    wtb, hidden, slope, dpre, left, tops, grads, *scratch = refs
+    strip = strips.shape[2]
+    fetched = [
+        pltpu.make_async_copy(
+            wl.at[:, strip * n : strip * n + strip], strips.at[n], strip_sem.at[n]
+        )
+        for n in range(strips.shape[0])
+    ]
+    for made in fetched:
+        made.start()
+    loads = load_all(stored, here, load_sem)
     chip, rep = place()
     barrier = pltpu.get_barrier_semaphore()
     for axis in range(3):
@@ -579,15 +624,21 @@
     pl.semaphore_signal(
         barrier, inc=1, device_id=(lax.axis_index("store"), 1 - rep), device_id_type=MESH
     )
-    step_part(scale, x, wl, wt_t, at_t, lab, logits_out, grads, wtb, hidden, slope, dpre, left)
+    for made in loads:
+        made.wait()
+    gradient_span = step_part(
+        scale, x, strips, fetched, wt_t, at_t, lab, logits_out, grads, wtb, hidden, slope, dpre, left, tops
+    )
     pl.semaphore_wait(barrier, 10)
-    reduce_part(chip, rep, grads, ml, vl, mt, vt, everyone, gradient_out, *scratch)
+    reduce_part(gradient_span, chip, rep, grads, ml, vl, mt, vt, everyone, gradient_out, *scratch)
 
 
 def train(x, weights_low, top_t, adjacency_t, labels, scale, ml, vl, mt, vt):
     near = x.shape[0]
     seeds = adjacency_t.shape[1]
     width = weights_low.shape[1]
+    given = (top_t, adjacency_t, labels, ml, vl, mt, vt)
+    hbm = pl.BlockSpec(memory_space=pltpu.MemorySpace.HBM)
     cube = (SIDE, SIDE, SIDE)
     tile = (16, width)
     vmem = pl.BlockSpec(memory_space=pltpu.VMEM)
@@ -599,14 +650,19 @@
             jax.ShapeDtypeStruct(cube + (2,) + tile, BF16),
             jax.ShapeDtypeStruct(tile, F32),
         ),
-        in_specs=[vmem] * 9,
+        in_specs=[vmem] + [hbm] * 8,
         out_specs=(vmem,) * 3,
-        scratch_shapes=[
+        scratch_shapes=[pltpu.VMEM(each.shape, each.dtype) for each in given]
+        + [
+            pltpu.SemaphoreType.DMA((len(given),)),
+            pltpu.VMEM((width // 256, weights_low.shape[0], 256), F32),
+            pltpu.SemaphoreType.DMA((width // 256,)),
             pltpu.VMEM((256, 2 * width), BF16),
             pltpu.VMEM((near, width), BF16),
             pltpu.VMEM((near, width), F32),
             pltpu.VMEM((near, width), BF16),
             pltpu.VMEM((2 * width, near), BF16),
+            pltpu.VMEM((width // 256, 2 * width, seeds), BF16),
             pltpu.VMEM(cube + (2,) + tile, BF16),
             pltpu.VMEM(cube + tile, BF16),
             pltpu.VMEM(cube + tile, BF16),
@@ -624,9 +680,9 @@
             pltpu.SemaphoreType.DMA((3, SIDE)),
         ],
         compiler_params=pltpu.CompilerParams(
-            collective_id=1, has_side_effects=True, vmem_limit_bytes=40 << 20
+            collective_id=1, has_side_effects=True, vmem_limit_bytes=44 << 20
         ),
-    )(x, weights_low, top_t, adjacency_t, labels, ml, vl, mt, vt)
+    )(x, weights_low, *given)
 
 
 def finish_kernel(
@@ -635,12 +691,10 @@
 ):
     classes = wt_t.shape[0]
     wl_out[...] = wl[...] - dot(spread_low(), steps[...])
-    for m in range(2):
-        rows = slice(256 * m, 256 * m + 256)
-        step = jnp.zeros((256, 256), F32)
-        for b in range(4):
-            step = step + dot(spread_top(b), steps[rows, 256 * b : 256 * b + 256])
-        wt_t_out[:, rows] = wt_t[:, rows] - jnp.transpose(step)[0:classes]
+    step = jnp.zeros((256, 256), F32)
+    for b in range(4):
+        step = step + dot(spread_top(b), steps[:, 256 * b : 256 * b + 256])
+    wt_t_out[...] = wt_t[...] - jnp.transpose(step)[0:classes]
 
     @pl.when(pl.program_id(0) == 0)
     def _():
@@ -653,19 +707,19 @@
 def finish(steps, gradient, logits, weights_low, top_t, ml, vl, mt, vt):
     rows, width = weights_low.shape
     classes, tops = top_t.shape
-    low = pl.BlockSpec((384, width), lambda i: (i, 0))
-    top = pl.BlockSpec((classes, 512), lambda i: (0, i))
+    low = pl.BlockSpec((192, width), lambda i: (i, 0))
+    top = pl.BlockSpec((classes, 256), lambda i: (0, i))
     same = [pl.BlockSpec(each.shape, lambda i: (0, 0)) for each in (ml, vl, mt, vt)]
     share = pl.BlockSpec(gradient.shape, lambda i: (0, 0))
     scores = pl.BlockSpec(logits.shape, lambda i: (0, 0))
     return pl.pallas_call(
         finish_kernel,
-        grid=(4,),
+        grid=(8,),
         out_shape=tuple(
             jax.ShapeDtypeStruct(each.shape, F32)
             for each in (logits, weights_low, top_t, ml, vl, mt, vt)
         ),
-        in_specs=[pl.BlockSpec((512, width), lambda i: (i, 0)), share, scores, low, top] + same,
+        in_specs=[pl.BlockSpec((256, width), lambda i: (i, 0)), share, scores, low, top] + same,
         out_specs=[scores, low, top] + same,
         scratch_shapes=[pltpu.VMEM((16, 256), F32)],
         compiler_params=pltpu.CompilerParams(vmem_limit_bytes=32 << 20),

time: 224 us -> 220 us (0.982)
  local copies, waits for them, and re-layouts: 4.23 us -> 1.44 us
    pallas_call x1, Pallas kernels: 156 us -> 152 us  [fetch(): pl.pallas_call(fetch_kernel, out_shape=jax.ShapeDtypeStruct((near, 2 * wi...]
    unnamed x22 -> x20, local copies, waits for them, and re-layouts: 4.23 us -> 1.44 us
where the time goes in v4:
time: 220 us
  Pallas kernels  218 us (99%)
    pallas_call x1, Pallas kernels, fetch(): pl.pallas_call(fetch_kernel, out_shape=jax.ShapeDtypeStruct((near, 2 * wi...  152 us
    pallas_call x1, Pallas kernels, train(): pl.pallas_call(functools.partial(train_kernel, scale), out_shape=(jax.Sha...  58.9 us
    pallas_call x1, Pallas kernels, finish(): pl.pallas_call(finish_kernel, grid=(8,), out_shape=tuple((jax.ShapeDtypeS...  6.45 us

profile of v4, /device:TPU:1, one launch (start us, length us, event | category | flops | bytes accessed | tf_op | source)
XLA Modules:
  0.0 220.1 jit_solution(5180432964666326750)
XLA Ops:
  0.6 0.0 copy-start.5
  0.6 0.0 copy-start.4
  0.7 0.0 copy-start.3
  0.7 0.0 copy-start.2
  0.7 0.0 copy-start.1
  0.7 0.0 copy-start.7
  0.7 0.0 copy-start.6
  0.7 0.0 slice-start
  0.7 152.3 %shard_map.198.x = bf16[512,1536]{1,0:T(8,128)(2,1)} custom-call(s32[1,512]{1,0:T(1,128)} %bitcast.21, s32[1,512]{1,0:T(1,128)} %bitcast.22, s32[1,3072]{1,0:T(1,128)} %bitcast.19, s32[1,3072]{1,0:T(1,128)} %bitcast.20, s32[15,512]{1,0:T(8,128)} %bitcast.18, f32[64,128]{1,0:T(8,128)} %constant.2.clone.spots, bf16[2048,768]{1,0:T(8,128)(2,1)} %feat.1), custom_call_target="tpu_custom_call" | custom-call | tf_op jit(solution)/shard_map/pallas_call | solution.py:297
  153.0 0.0 copy-done.5
  153.0 0.0 copy-done.4
  153.1 0.0 copy-done.3
  153.1 0.0 copy-done.2
  153.1 0.0 copy-done.1
  153.1 0.0 copy-done.7
  153.1 0.0 copy-done.6
  153.1 0.0 copy-start
  153.1 1.4 copy-done
  154.5 0.0 slice-start.1
  154.5 58.9 %shard_map.199 = (f32[153,128]{1,0:T(8,128)S(1)}, bf16[4,4,4,2,16,1024]{5,4,3,2,1,0:T(8,128)(2,1)S(1)}, f32[16,1024]{1,0:T(8,128)S(1)}) custom-call(bf16[512,1536]{1,0:T(8,128)(2,1)S(1)} %copy-done, f32[1536,1024]{1,0:T(8,128)} %wl.3, f32[153,2048]{1,0:T(8,128)S(1)} %bitcast.13, s32[10,128]{1,0:T(8,128)S(1)} %bitcast.16, s32[1,128]{1,0:T(1,128)S(1)} %bitcast.17, ...), custom_call_target="tpu_custom_call" | custom-call | tf_op jit(solution)/shard_map/pallas_call | solution.py:646
  213.4 0.0 slice-done
  213.4 0.0 slice-done.1
  213.4 6.5 %shard_map.200 = (f32[153,128]{1,0:T(8,128)}, f32[1536,1024]{1,0:T(8,128)}, f32[153,2048]{1,0:T(8,128)}, f32[12,1024]{1,0:T(8,128)}, f32[12,1024]{1,0:T(8,128)}, /*index=5*/f32[16,153]{1,0:T(8,128)}, f32[16,153]{1,0:T(8,128)}) custom-call(bf16[2048,1024]{1,0:T(8,128)(2,1)S(1)} %bitcast.15, f32[16,1024]{1,0:T(8,128)S(1)} %get-tuple-element.18.gradient, ...), custom_call_target="tpu_custom_call" | custom-call | tf_op jit(solution)/shard_map/pallas_call | solution.py:715
  (1 shorter events, 0.0 us)
Async XLA Ops:
  0.6 152.4 %copy-start.5 = (f32[16,153]{1,0:T(8,128)S(1)}, f32[16,153]{1,0:T(8,128)}, u32[]{:S(2)}) copy-start(f32[16,153]{1,0:T(8,128)} %vt.1) | copy-start | bytes 29380
  0.6 152.4 %copy-start.4 = (f32[16,153]{1,0:T(8,128)S(1)}, f32[16,153]{1,0:T(8,128)}, u32[]{:S(2)}) copy-start(f32[16,153]{1,0:T(8,128)} %mt.1) | copy-start | bytes 29380
  0.7 152.4 %copy-start.3 = (f32[12,1024]{1,0:T(8,128)S(1)}, f32[12,1024]{1,0:T(8,128)}, u32[]{:S(2)}) copy-start(f32[12,1024]{1,0:T(8,128)} %vl.1) | copy-start | bytes 147460
  0.7 152.4 %copy-start.2 = (f32[12,1024]{1,0:T(8,128)S(1)}, f32[12,1024]{1,0:T(8,128)}, u32[]{:S(2)}) copy-start(f32[12,1024]{1,0:T(8,128)} %ml.1) | copy-start | bytes 147460
  0.7 152.4 %copy-start.1 = (f32[2048,153]{0,1:T(8,128)S(1)}, f32[2048,153]{0,1:T(8,128)}, u32[]{:S(2)}) copy-start(f32[2048,153]{0,1:T(8,128)} %param.24) | copy-start | bytes 3760132
  0.7 152.4 %copy-start.7 = (s32[128]{0:T(128)S(1)}, s32[128]{0:T(128)}, u32[]{:S(2)}) copy-start(s32[128]{0:T(128)} %param.22) | copy-start | bytes 1540
  0.7 152.4 %copy-start.6 = (s32[128,10]{0,1:T(8,128)S(1)}, s32[128,10]{0,1:T(8,128)}, u32[]{:S(2)}) copy-start(s32[128,10]{0,1:T(8,128)} %param.21) | copy-start | bytes 15364
  0.7 212.7 %slice-start = ((s8[6291456]{0:T(1024)(128)(4,1)}), s8[2097152]{0:T(1024)(128)(4,1)S(1)}, s32[]{:S(2)}) async-start(s8[6291456]{0:T(1024)(128)(4,1)} %bitcast.11), calls=%async_computation | async-start | bytes 4194304
  153.1 1.4 copy-start
  154.5 58.9 %slice-start.1 = ((s8[6291456]{0:T(1024)(128)(4,1)}), s8[4194304]{0:T(1024)(128)(4,1)S(1)}, s32[]{:S(2)}) async-start(s8[6291456]{0:T(1024)(128)(4,1)} %bitcast.11), calls=%async_computation.1 | async-start | bytes 8388608

commit v5 on v4

--- a/solution.py
+++ b/solution.py
@@ -49,9 +49,13 @@
     return [lax.rem(c + step, SIDE) if n == axis else c for n, c in enumerate(chip)]
 
 
-def partner(shift, chip, sign):
-    steps = (shift // 16, lax.rem(shift // 4, 4), lax.rem(shift, 4))
-    return at([lax.rem(c + sign * step + SIDE, SIDE) for c, step in zip(chip, steps)])
+def each_shift(chip, sign, act):
+    x, y, z = [
+        [lax.rem(c + sign * step + SIDE, SIDE) * scale for step in range(SIDE)]
+        for c, scale in zip(chip, (SIDE * SIDE, SIDE, 1))
+    ]
+    for shift in range(1, STORES):
+        act(shift, x[shift // 16] + y[shift // 4 % 4] + z[shift % 4])
 
 
 def routes():
@@ -103,11 +107,10 @@
     chip, rep = place()
     barrier = pltpu.get_barrier_semaphore()
 
-    @pl.loop(1, STORES)
-    def _(shift):
-        pl.semaphore_signal(
-            barrier, inc=1, device_id=(partner(shift, chip, 1), rep), device_id_type=MESH
-        )
+    def greet(shift, store):
+        pl.semaphore_signal(barrier, inc=1, device_id=(store, rep), device_id_type=MESH)
+
+    each_shift(chip, 1, greet)
 
     table[...] = jnp.zeros_like(table)
     upper = (iota((256, 256), 0) < iota((256, 256), 1)).astype(BF16)
@@ -150,16 +153,17 @@
 
     pl.semaphore_wait(barrier, STORES - 1)
 
-    def ask(shift):
-        return pltpu.make_async_remote_copy(
+    asks = []
+
+    def ask(shift, store):
+        asks.append(pltpu.make_async_remote_copy(
             src_ref=req_out.at[shift], dst_ref=req_in.at[shift],
             send_sem=ask_send.at[shift], recv_sem=ask_recv.at[shift],
-            device_id=(partner(shift, chip, -1), rep), device_id_type=MESH,
-        )
-
-    @pl.loop(1, STORES)
-    def _(shift):
-        ask(shift).start()
+            device_id=(store, rep), device_id_type=MESH,
+        ))
+        asks[-1].start()
+
+    each_shift(chip, -1, ask)
 
     table_t = jnp.transpose(table[...]).astype(BF16)
     fan = adj.shape[0]
@@ -175,10 +179,8 @@
         block = slice(128 * c, 128 * c + 128)
         chosen[block, :] = jnp.transpose(cols[:, block])
 
-    @pl.loop(1, STORES)
-    def _(shift):
-        ask(shift).wait()
-
+    for made in asks:
+        made.wait_recv()
     lists = jnp.concatenate(
         [req_in[shift].astype(F32) for shift in LEAVE] + [jnp.zeros((64, 128), F32)], axis=0
     )
@@ -202,7 +204,7 @@
             dst = relay_two.at[LEAVE.index(shift)]
         hops[shift, hop] = pltpu.make_async_remote_copy(
             src_ref=src, dst_ref=dst,
-            send_sem=(send_one, send_two, send_three)[hop].at[shift],
+            send_sem=(send_one, send_two, send_three)[hop].at[LEAVE.index(shift)],
             recv_sem=(recv_one, recv_two, recv_three)[hop].at[shift],
             device_id=(at(moved(chip, *route[hop])), rep), device_id_type=MESH,
         )
@@ -283,8 +285,19 @@
                 out[:, features + 256 * h : features + 256 * h + 256] = (
                     sums / float(fan)
                 ).astype(BF16)
-    for made in hops.values():
-        made.wait_send()
+
+    def sent(src, sem, begin, end):
+        @pl.loop(begin, end)
+        def _(n):
+            pltpu.make_async_remote_copy(
+                src_ref=src.at[n], dst_ref=src.at[n], send_sem=sem.at[n], recv_sem=sem.at[n],
+                device_id=(at(moved(chip, 0, 1)), rep), device_id_type=MESH,
+            ).wait_send()
+
+    sent(req_out, ask_send, 1, STORES)
+    sent(send, send_one, 0, STORES - 1)
+    sent(relay_one, send_two, 0, len(THREE) + len(TWO))
+    sent(relay_two, send_three, 0, len(THREE))
 
 
 def fetch(owners_near, slots_near, owners_far, slots_far, adjacency, features):
@@ -369,6 +382,9 @@
     near = x.shape[0]
     wtb[...] = jnp.zeros_like(wtb)
     wtb[0:classes, :] = wt_t[...].astype(BF16)
+    low_t = spread_low_t()
+    for m in range(x.shape[1] // 384):
+        left[512 * m : 512 * m + 512, :] = dot_nt(low_t, x[:, 384 * m : 384 * m + 384]).astype(BF16)
     for n in range(width // 256):
         span = slice(256 * n, 256 * n + 256)
         fetched[n].wait()
@@ -398,9 +414,6 @@
         back = dot(picks_t, second_high[:, span]) + dot(picks_t, second_low[:, span])
         dpre[seeds:near, span] = (back[seeds:near] * slope[seeds:near, span]).astype(BF16)
         dpre[0:seeds, span] = ((back[0:seeds] + first[:, span]) * slope[0:seeds, span]).astype(BF16)
-    low_t = spread_low_t()
-    for m in range(x.shape[1] // 384):
-        left[512 * m : 512 * m + 512, :] = dot_nt(low_t, x[:, 384 * m : 384 * m + 384]).astype(BF16)
     for b in range(width // 256):
         top_t = spread_top_t(b)
         for m in range(2 * width // 256):
@@ -508,13 +521,16 @@
         left = tuple(n for n in range(3) if n != first)
         for made in waiting[c]:
             made.wait_recv()
-        for a in range(SIDE):
+
+        @pl.loop(0, SIDE)
+        def _(a):
             for b in range(SIDE):
                 spot = {left[0]: a, left[1]: b, first: chip[first]}
                 total = halves[block_of((0, 1, 2), spot, (every, span))].astype(F32)
                 for k in range(1, SIDE):
                     total = total + got_one[k - 1, a, b, :, span].astype(F32)
                 sum_one[a, b, :, span] = total.astype(BF16)
+
         copies = []
         for k in range(1, SIDE):
             to = moved(chip, second, k)
@@ -687,13 +703,20 @@
 
 def finish_kernel(
     steps, gradient, logits, wl, wt_t, ml, vl, mt, vt,
-    logits_out, wl_out, wt_t_out, ml_out, vl_out, mt_out, vt_out, top,
+    logits_out, wl_out, wt_t_out, ml_out, vl_out, mt_out, vt_out, top, low_rows, top_rows_of,
 ):
     classes = wt_t.shape[0]
-    wl_out[...] = wl[...] - dot(spread_low(), steps[...])
+
+    @pl.when(pl.program_id(0) == 0)
+    def _():
+        low_rows[...] = spread_low()
+        for b in range(4):
+            top_rows_of[b] = spread_top(b)
+
+    wl_out[...] = wl[...] - dot(low_rows[...], steps[...])
     step = jnp.zeros((256, 256), F32)
     for b in range(4):
-        step = step + dot(spread_top(b), steps[:, 256 * b : 256 * b + 256])
+        step = step + dot(top_rows_of[b], steps[:, 256 * b : 256 * b + 256])
     wt_t_out[...] = wt_t[...] - jnp.transpose(step)[0:classes]
 
     @pl.when(pl.program_id(0) == 0)
@@ -721,7 +744,11 @@
         ),
         in_specs=[pl.BlockSpec((256, width), lambda i: (i, 0)), share, scores, low, top] + same,
         out_specs=[scores, low, top] + same,
-        scratch_shapes=[pltpu.VMEM((16, 256), F32)],
+        scratch_shapes=[
+            pltpu.VMEM((16, 256), F32),
+            pltpu.VMEM((192, 256), BF16),
+            pltpu.VMEM((4, 256, 256), BF16),
+        ],
         compiler_params=pltpu.CompilerParams(vmem_limit_bytes=32 << 20),
     )(steps, gradient, logits, weights_low, top_t, ml, vl, mt, vt)
 

time: 220 us -> 220 us (level)
  no operation moved by 1% of the time
where the time goes in v5:
time: 220 us
  Pallas kernels  217 us (99%)
    pallas_call x1, Pallas kernels, fetch(): pl.pallas_call(fetch_kernel, out_shape=jax.ShapeDtypeStruct((near, 2 * wi...  152 us
    pallas_call x1, Pallas kernels, train(): pl.pallas_call(functools.partial(train_kernel, scale), out_shape=(jax.Sha...  58.8 us
    pallas_call x1, Pallas kernels, finish(): pl.pallas_call(finish_kernel, grid=(8,), out_shape=tuple((jax.ShapeDtypeS...  6.55 us

profile of v5, /device:TPU:1, one launch (start us, length us, event | category | flops | bytes accessed | tf_op | source)
XLA Modules:
  0.0 219.5 jit_solution(4430894150011764457)
XLA Ops:
  0.6 0.0 copy-start.5
  0.6 0.0 copy-start.4
  0.7 0.0 copy-start.3
  0.7 0.0 copy-start.2
  0.7 0.0 copy-start.1
  0.7 0.0 copy-start.7
  0.7 0.0 copy-start.6
  0.7 0.0 slice-start
  0.7 151.8 %shard_map.198.x = bf16[512,1536]{1,0:T(8,128)(2,1)} custom-call(s32[1,512]{1,0:T(1,128)} %bitcast.21, s32[1,512]{1,0:T(1,128)} %bitcast.22, s32[1,3072]{1,0:T(1,128)} %bitcast.19, s32[1,3072]{1,0:T(1,128)} %bitcast.20, s32[15,512]{1,0:T(8,128)} %bitcast.18, f32[64,128]{1,0:T(8,128)} %constant.2.clone.spots, bf16[2048,768]{1,0:T(8,128)(2,1)} %feat.1), custom_call_target="tpu_custom_call" | custom-call | tf_op jit(solution)/shard_map/pallas_call | solution.py:310
  152.5 0.0 copy-done.5
  152.5 0.0 copy-done.4
  152.5 0.0 copy-done.3
  152.5 0.0 copy-done.2
  152.5 0.0 copy-done.1
  152.5 0.0 copy-done.7
  152.6 0.0 copy-done.6
  152.6 0.0 copy-start
  152.6 1.4 copy-done
  154.0 0.0 slice-start.1
  154.0 58.8 %shard_map.199 = (f32[153,128]{1,0:T(8,128)S(1)}, bf16[4,4,4,2,16,1024]{5,4,3,2,1,0:T(8,128)(2,1)S(1)}, f32[16,1024]{1,0:T(8,128)S(1)}) custom-call(bf16[512,1536]{1,0:T(8,128)(2,1)S(1)} %copy-done, f32[1536,1024]{1,0:T(8,128)} %wl.3, f32[153,2048]{1,0:T(8,128)S(1)} %bitcast.13, s32[10,128]{1,0:T(8,128)S(1)} %bitcast.16, s32[1,128]{1,0:T(1,128)S(1)} %bitcast.17, ...), custom_call_target="tpu_custom_call" | custom-call | tf_op jit(solution)/shard_map/pallas_call | solution.py:662
  212.8 0.0 slice-done
  212.8 0.0 slice-done.1
  212.8 6.5 %shard_map.200 = (f32[153,128]{1,0:T(8,128)}, f32[1536,1024]{1,0:T(8,128)}, f32[153,2048]{1,0:T(8,128)}, f32[12,1024]{1,0:T(8,128)}, f32[12,1024]{1,0:T(8,128)}, /*index=5*/f32[16,153]{1,0:T(8,128)}, f32[16,153]{1,0:T(8,128)}) custom-call(bf16[2048,1024]{1,0:T(8,128)(2,1)S(1)} %bitcast.15, f32[16,1024]{1,0:T(8,128)S(1)} %get-tuple-element.18.gradient, ...), custom_call_target="tpu_custom_call" | custom-call | tf_op jit(solution)/shard_map/pallas_call | solution.py:738
  (1 shorter events, 0.0 us)
Async XLA Ops:
  0.6 151.9 %copy-start.5 = (f32[16,153]{1,0:T(8,128)S(1)}, f32[16,153]{1,0:T(8,128)}, u32[]{:S(2)}) copy-start(f32[16,153]{1,0:T(8,128)} %vt.1) | copy-start | bytes 29380
  0.6 151.9 %copy-start.4 = (f32[16,153]{1,0:T(8,128)S(1)}, f32[16,153]{1,0:T(8,128)}, u32[]{:S(2)}) copy-start(f32[16,153]{1,0:T(8,128)} %mt.1) | copy-start | bytes 29380
  0.7 151.9 %copy-start.3 = (f32[12,1024]{1,0:T(8,128)S(1)}, f32[12,1024]{1,0:T(8,128)}, u32[]{:S(2)}) copy-start(f32[12,1024]{1,0:T(8,128)} %vl.1) | copy-start | bytes 147460
  0.7 151.9 %copy-start.2 = (f32[12,1024]{1,0:T(8,128)S(1)}, f32[12,1024]{1,0:T(8,128)}, u32[]{:S(2)}) copy-start(f32[12,1024]{1,0:T(8,128)} %ml.1) | copy-start | bytes 147460
  0.7 151.9 %copy-start.1 = (f32[2048,153]{0,1:T(8,128)S(1)}, f32[2048,153]{0,1:T(8,128)}, u32[]{:S(2)}) copy-start(f32[2048,153]{0,1:T(8,128)} %param.24) | copy-start | bytes 3760132
  0.7 151.9 %copy-start.7 = (s32[128]{0:T(128)S(1)}, s32[128]{0:T(128)}, u32[]{:S(2)}) copy-start(s32[128]{0:T(128)} %param.22) | copy-start | bytes 1540
  0.7 151.9 %copy-start.6 = (s32[128,10]{0,1:T(8,128)S(1)}, s32[128,10]{0,1:T(8,128)}, u32[]{:S(2)}) copy-start(s32[128,10]{0,1:T(8,128)} %param.21) | copy-start | bytes 15364
  0.7 212.1 %slice-start = ((s8[6291456]{0:T(1024)(128)(4,1)}), s8[2097152]{0:T(1024)(128)(4,1)S(1)}, s32[]{:S(2)}) async-start(s8[6291456]{0:T(1024)(128)(4,1)} %bitcast.11), calls=%async_computation | async-start | bytes 4194304
  152.6 1.4 copy-start
  154.0 58.8 %slice-start.1 = ((s8[6291456]{0:T(1024)(128)(4,1)}), s8[4194304]{0:T(1024)(128)(4,1)S(1)}, s32[]{:S(2)}) async-start(s8[6291456]{0:T(1024)(128)(4,1)} %bitcast.11), calls=%async_computation.1 | async-start | bytes 8388608

commit v6 on v5

--- a/solution.py
+++ b/solution.py
@@ -49,13 +49,16 @@
     return [lax.rem(c + step, SIDE) if n == axis else c for n, c in enumerate(chip)]
 
 
-def each_shift(chip, sign, act):
+PLANE = SIDE * SIDE
+
+
+def peers(chip, sign):
     x, y, z = [
         [lax.rem(c + sign * step + SIDE, SIDE) * scale for step in range(SIDE)]
-        for c, scale in zip(chip, (SIDE * SIDE, SIDE, 1))
+        for c, scale in zip(chip, (PLANE, SIDE, 1))
     ]
-    for shift in range(1, STORES):
-        act(shift, x[shift // 16] + y[shift // 4 % 4] + z[shift % 4])
+    line = [x[step] + y[0] + z[0] for step in range(SIDE)]
+    return line, [x[0] + y[step // SIDE] + z[step % SIDE] for step in range(PLANE)]
 
 
 def routes():
@@ -100,17 +103,16 @@
 
 def fetch_kernel(
     own_near, slot_near, own_far, slot_far, adj, spots, feat, out,
-    table, cols, chosen, req_out, req_in, asked, counts, selves, send, relay_one, relay_two, recv,
+    table, cols, chosen, req_out, req_mid, req_in, asked, counts, selves, send, relay_one, relay_two, recv,
     total, marks,
-    ask_send, ask_recv, send_one, send_two, send_three, recv_one, recv_two, recv_three,
+    mid_send, mid_recv, ask_send, ask_recv, send_one, send_two, send_three, recv_one, recv_two, recv_three,
 ):
     chip, rep = place()
     barrier = pltpu.get_barrier_semaphore()
 
-    def greet(shift, store):
+    line, plane = peers(chip, 1)
+    for store in line[1:] + plane[1:]:
         pl.semaphore_signal(barrier, inc=1, device_id=(store, rep), device_id_type=MESH)
-
-    each_shift(chip, 1, greet)
 
     table[...] = jnp.zeros_like(table)
     upper = (iota((256, 256), 0) < iota((256, 256), 1)).astype(BF16)
@@ -120,7 +122,9 @@
     near_rows = own_near.shape[1]
     near_blocks = near_rows // 256
     spot = spots[:, 0:1]
-    for b in range(near_blocks + own_far.shape[1] // 256):
+    blocks = range(near_blocks + own_far.shape[1] // 256)
+    marked = []
+    for b in blocks:
         far = b >= near_blocks
         if b == near_blocks:
             base = jnp.zeros((STORES, 1), F32)
@@ -135,6 +139,10 @@
         owned_bf = owned.astype(BF16)
         before = dot(owned_bf, upper) + base
         base = base + jnp.sum(owned, axis=1, keepdims=True)
+        marked.append((wanted, owned, owned_bf, before))
+    positions = []
+    for b, (wanted, owned, owned_bf, before) in zip(blocks, marked):
+        far = b >= near_blocks
         position = jnp.sum(owned * before, axis=0, keepdims=True)
         if far:
             position = position + CAP_NEAR
@@ -143,32 +151,48 @@
             part = slice(128 * half, 128 * half + 128)
             table[2 * b + half : 2 * b + half + 1, 0:128] = arrival[:, part]
             table[2 * b + half : 2 * b + half + 1, 128:256] = position[:, part]
+        positions.append(position)
+    for (wanted, owned, owned_bf, before), position in zip(marked, positions):
         placed = (iota((128, 256), 0) == position.astype(jnp.int32)).astype(F32)
         high = high + dot_nt(owned_bf, (placed * (wanted >> 6).astype(F32)).astype(BF16))
         low = low + dot_nt(owned_bf, (placed * (wanted & 63).astype(F32)).astype(BF16))
     requests = (high * 64.0 + low).astype(jnp.int32)
     for shift in range(STORES):
-        req_out[shift] = requests[shift : shift + 1, :]
-    req_in[0] = requests[0:1, :]
-
-    pl.semaphore_wait(barrier, STORES - 1)
-
-    asks = []
-
-    def ask(shift, store):
-        asks.append(pltpu.make_async_remote_copy(
-            src_ref=req_out.at[shift], dst_ref=req_in.at[shift],
-            send_sem=ask_send.at[shift], recv_sem=ask_recv.at[shift],
+        held = req_out if shift >= PLANE else req_mid
+        held[shift // PLANE, shift % PLANE] = requests[shift : shift + 1, :]
+
+    pl.semaphore_wait(barrier, SIDE - 1 + PLANE - 1)
+
+    line, plane = peers(chip, -1)
+
+    def ask(src, dst, send_sem, recv_sem, store):
+        made = pltpu.make_async_remote_copy(
+            src_ref=src, dst_ref=dst, send_sem=send_sem, recv_sem=recv_sem,
             device_id=(store, rep), device_id_type=MESH,
-        ))
-        asks[-1].start()
-
-    each_shift(chip, -1, ask)
+        )
+        made.start()
+        return made
+
+    asks = [
+        ask(req_out.at[step], req_mid.at[step], mid_send.at[step], mid_recv.at[step], line[step])
+        for step in range(1, SIDE)
+    ]
 
     table_t = jnp.transpose(table[...]).astype(BF16)
     fan = adj.shape[0]
     cols[...] = jnp.zeros_like(cols)
     for k in range(fan + 1):
+        if k == fan // 2:
+            for made in asks:
+                made.wait_recv()
+            asks += [
+                ask(
+                    req_mid.at[:, step], req_in.at[:, step],
+                    ask_send.at[step], ask_recv.at[step], plane[step],
+                )
+                for step in range(1, PLANE)
+            ]
+            req_in[:, 0] = req_mid[:, 0]
         entry = adj[k : k + 1, :] if k < fan else iota((1, near_rows), 1)
         row_mark = (iota((128, near_rows), 0) == (entry >> 7)).astype(F32).astype(BF16)
         found = dot(table_t, row_mark)
@@ -179,10 +203,10 @@
         block = slice(128 * c, 128 * c + 128)
         chosen[block, :] = jnp.transpose(cols[:, block])
 
-    for made in asks:
+    for made in asks[SIDE - 1 :]:
         made.wait_recv()
     lists = jnp.concatenate(
-        [req_in[shift].astype(F32) for shift in LEAVE] + [jnp.zeros((64, 128), F32)], axis=0
+        [req_in[shift // PLANE, shift % PLANE].astype(F32) for shift in LEAVE] + [jnp.zeros((64, 128), F32)], axis=0
     )
     asked[...] = jnp.transpose(lists)[0:CAP, :]
 
@@ -294,7 +318,8 @@
                 device_id=(at(moved(chip, 0, 1)), rep), device_id_type=MESH,
             ).wait_send()
 
-    sent(req_out, ask_send, 1, STORES)
+    for made in asks:
+        made.wait_send()
     sent(send, send_one, 0, STORES - 1)
     sent(relay_one, send_two, 0, len(THREE) + len(TWO))
     sent(relay_two, send_three, 0, len(THREE))
@@ -316,8 +341,9 @@
             pltpu.VMEM((128, 256), F32),
             pltpu.VMEM((128, near), F32),
             pltpu.VMEM((near, 128), F32),
-            pltpu.VMEM((STORES, 1, 128), jnp.int32),
-            pltpu.VMEM((STORES, 1, 128), jnp.int32),
+            pltpu.VMEM((SIDE, PLANE, 1, 128), jnp.int32),
+            pltpu.VMEM((SIDE, PLANE, 1, 128), jnp.int32),
+            pltpu.VMEM((SIDE, PLANE, 1, 128), jnp.int32),
             pltpu.VMEM((CAP, 128), F32),
             pltpu.VMEM((GROUPS, near, STORES // GROUPS * CAP), BF16),
             pltpu.VMEM((GROUPS, near, 128), BF16),
@@ -327,7 +353,11 @@
             pltpu.VMEM((STORES,) + rows, BF16),
             pltpu.VMEM((near, width), F32),
             pltpu.VMEM((4 * CAP, features.shape[0]), BF16),
-            many, many, many, many, many, many, many, many,
+            pltpu.SemaphoreType.DMA((SIDE,)),
+            pltpu.SemaphoreType.DMA((SIDE,)),
+            pltpu.SemaphoreType.DMA((PLANE,)),
+            pltpu.SemaphoreType.DMA((PLANE,)),
+            many, many, many, many, many, many,
         ],
         compiler_params=pltpu.CompilerParams(
             collective_id=0, has_side_effects=True, vmem_limit_bytes=60 << 20
@@ -336,7 +366,7 @@
 
 
 def spread_low():
-    row, column = iota((192, 256), 0), iota((192, 256), 1)
+    row, column = iota((384, 512), 0), iota((384, 512), 1)
     inner = column & 15
     return ((inner < 12) & (row == 12 * (column >> 4) + inner)).astype(F32).astype(BF16)
 
@@ -714,10 +744,12 @@
             top_rows_of[b] = spread_top(b)
 
     wl_out[...] = wl[...] - dot(low_rows[...], steps[...])
-    step = jnp.zeros((256, 256), F32)
-    for b in range(4):
-        step = step + dot(top_rows_of[b], steps[:, 256 * b : 256 * b + 256])
-    wt_t_out[...] = wt_t[...] - jnp.transpose(step)[0:classes]
+    for m in range(2):
+        rows = slice(256 * m, 256 * m + 256)
+        step = jnp.zeros((256, 256), F32)
+        for b in range(4):
+            step = step + dot(top_rows_of[b], steps[rows, 256 * b : 256 * b + 256])
+        wt_t_out[:, rows] = wt_t[:, rows] - jnp.transpose(step)[0:classes]
 
     @pl.when(pl.program_id(0) == 0)
     def _():
@@ -730,23 +762,23 @@
 def finish(steps, gradient, logits, weights_low, top_t, ml, vl, mt, vt):
     rows, width = weights_low.shape
     classes, tops = top_t.shape
-    low = pl.BlockSpec((192, width), lambda i: (i, 0))
-    top = pl.BlockSpec((classes, 256), lambda i: (0, i))
+    low = pl.BlockSpec((384, width), lambda i: (i, 0))
+    top = pl.BlockSpec((classes, 512), lambda i: (0, i))
     same = [pl.BlockSpec(each.shape, lambda i: (0, 0)) for each in (ml, vl, mt, vt)]
     share = pl.BlockSpec(gradient.shape, lambda i: (0, 0))
     scores = pl.BlockSpec(logits.shape, lambda i: (0, 0))
     return pl.pallas_call(
         finish_kernel,
-        grid=(8,),
+        grid=(4,),
         out_shape=tuple(
             jax.ShapeDtypeStruct(each.shape, F32)
             for each in (logits, weights_low, top_t, ml, vl, mt, vt)
         ),
-        in_specs=[pl.BlockSpec((256, width), lambda i: (i, 0)), share, scores, low, top] + same,
+        in_specs=[pl.BlockSpec((512, width), lambda i: (i, 0)), share, scores, low, top] + same,
         out_specs=[scores, low, top] + same,
         scratch_shapes=[
             pltpu.VMEM((16, 256), F32),
-            pltpu.VMEM((192, 256), BF16),
+            pltpu.VMEM((384, 512), BF16),
             pltpu.VMEM((4, 256, 256), BF16),
         ],
         compiler_params=pltpu.CompilerParams(vmem_limit_bytes=32 << 20),

time: 220 us -> 217 us (0.986)
    pallas_call x1, Pallas kernels: 152 us -> 149 us  [fetch(): pl.pallas_call(fetch_kernel, out_shape=jax.ShapeDtypeStruct((near, 2 * wi...]
where the time goes in v6:
time: 217 us
  Pallas kernels  215 us (99%)
    pallas_call x1, Pallas kernels, fetch(): pl.pallas_call(fetch_kernel, out_shape=jax.ShapeDtypeStruct((near, 2 * wi...  149 us
    pallas_call x1, Pallas kernels, train(): pl.pallas_call(functools.partial(train_kernel, scale), out_shape=(jax.Sha...  59.6 us
    pallas_call x1, Pallas kernels, finish(): pl.pallas_call(finish_kernel, grid=(4,), out_shape=tuple((jax.ShapeDtypeS...  6.01 us

profile of v6, /device:TPU:1, one launch (start us, length us, event | category | flops | bytes accessed | tf_op | source)
XLA Modules:
  0.0 217.1 jit_solution(5830238118640865406)
XLA Ops:
  0.6 0.0 copy-start.5
  0.6 0.0 copy-start.4
  0.7 0.0 copy-start.3
  0.7 0.0 copy-start.2
  0.7 0.0 copy-start.1
  0.7 0.0 copy-start.7
  0.7 0.0 copy-start.6
  0.7 0.0 slice-start
  0.7 149.1 %shard_map.198.x = bf16[512,1536]{1,0:T(8,128)(2,1)} custom-call(s32[1,512]{1,0:T(1,128)} %bitcast.21, s32[1,512]{1,0:T(1,128)} %bitcast.22, s32[1,3072]{1,0:T(1,128)} %bitcast.19, s32[1,3072]{1,0:T(1,128)} %bitcast.20, s32[15,512]{1,0:T(8,128)} %bitcast.18, f32[64,128]{1,0:T(8,128)} %constant.2.clone.spots, bf16[2048,768]{1,0:T(8,128)(2,1)} %feat.1), custom_call_target="tpu_custom_call" | custom-call | tf_op jit(solution)/shard_map/pallas_call | solution.py:335
  149.8 0.0 copy-done.5
  149.8 0.0 copy-done.4
  149.8 0.0 copy-done.3
  149.8 0.0 copy-done.2
  149.8 0.0 copy-done.1
  149.8 0.0 copy-done.7
  149.9 0.0 copy-done.6
  149.9 0.0 copy-start
  149.9 1.4 copy-done
  151.3 0.0 slice-start.1
  151.3 59.6 %shard_map.199 = (f32[153,128]{1,0:T(8,128)S(1)}, bf16[4,4,4,2,16,1024]{5,4,3,2,1,0:T(8,128)(2,1)S(1)}, f32[16,1024]{1,0:T(8,128)S(1)}) custom-call(bf16[512,1536]{1,0:T(8,128)(2,1)S(1)} %copy-done, f32[1536,1024]{1,0:T(8,128)} %wl.3, f32[153,2048]{1,0:T(8,128)S(1)} %bitcast.13, s32[10,128]{1,0:T(8,128)S(1)} %bitcast.16, s32[1,128]{1,0:T(1,128)S(1)} %bitcast.17, ...), custom_call_target="tpu_custom_call" | custom-call | tf_op jit(solution)/shard_map/pallas_call | solution.py:692
  210.9 0.0 slice-done
  210.9 0.0 slice-done.1
  210.9 6.0 %shard_map.200 = (f32[153,128]{1,0:T(8,128)}, f32[1536,1024]{1,0:T(8,128)}, f32[153,2048]{1,0:T(8,128)}, f32[12,1024]{1,0:T(8,128)}, f32[12,1024]{1,0:T(8,128)}, /*index=5*/f32[16,153]{1,0:T(8,128)}, f32[16,153]{1,0:T(8,128)}) custom-call(bf16[2048,1024]{1,0:T(8,128)(2,1)S(1)} %bitcast.15, f32[16,1024]{1,0:T(8,128)S(1)} %get-tuple-element.18.gradient, ...), custom_call_target="tpu_custom_call" | custom-call | tf_op jit(solution)/shard_map/pallas_call | solution.py:770
  (1 shorter events, 0.0 us)
Async XLA Ops:
  0.6 149.2 %copy-start.5 = (f32[16,153]{1,0:T(8,128)S(1)}, f32[16,153]{1,0:T(8,128)}, u32[]{:S(2)}) copy-start(f32[16,153]{1,0:T(8,128)} %vt.1) | copy-start | bytes 29380
  0.6 149.2 %copy-start.4 = (f32[16,153]{1,0:T(8,128)S(1)}, f32[16,153]{1,0:T(8,128)}, u32[]{:S(2)}) copy-start(f32[16,153]{1,0:T(8,128)} %mt.1) | copy-start | bytes 29380
  0.7 149.2 %copy-start.3 = (f32[12,1024]{1,0:T(8,128)S(1)}, f32[12,1024]{1,0:T(8,128)}, u32[]{:S(2)}) copy-start(f32[12,1024]{1,0:T(8,128)} %vl.1) | copy-start | bytes 147460
  0.7 149.2 %copy-start.2 = (f32[12,1024]{1,0:T(8,128)S(1)}, f32[12,1024]{1,0:T(8,128)}, u32[]{:S(2)}) copy-start(f32[12,1024]{1,0:T(8,128)} %ml.1) | copy-start | bytes 147460
  0.7 149.2 %copy-start.1 = (f32[2048,153]{0,1:T(8,128)S(1)}, f32[2048,153]{0,1:T(8,128)}, u32[]{:S(2)}) copy-start(f32[2048,153]{0,1:T(8,128)} %param.24) | copy-start | bytes 3760132
  0.7 149.2 %copy-start.7 = (s32[128]{0:T(128)S(1)}, s32[128]{0:T(128)}, u32[]{:S(2)}) copy-start(s32[128]{0:T(128)} %param.22) | copy-start | bytes 1540
  0.7 149.2 %copy-start.6 = (s32[128,10]{0,1:T(8,128)S(1)}, s32[128,10]{0,1:T(8,128)}, u32[]{:S(2)}) copy-start(s32[128,10]{0,1:T(8,128)} %param.21) | copy-start | bytes 15364
  0.7 210.2 %slice-start = ((s8[6291456]{0:T(1024)(128)(4,1)}), s8[2097152]{0:T(1024)(128)(4,1)S(1)}, s32[]{:S(2)}) async-start(s8[6291456]{0:T(1024)(128)(4,1)} %bitcast.11), calls=%async_computation | async-start | bytes 4194304
  149.9 1.4 copy-start
  151.3 59.6 %slice-start.1 = ((s8[6291456]{0:T(1024)(128)(4,1)}), s8[4194304]{0:T(1024)(128)(4,1)S(1)}, s32[]{:S(2)}) async-start(s8[6291456]{0:T(1024)(128)(4,1)} %bitcast.11), calls=%async_computation.1 | async-start | bytes 8388608
